TPU v7x, 32 devices: a whole 2x2x4 slice. The times are simulated.
32 devices in a mesh: dp: 8 (over y, x, core), tensor: 4 (over z).
Axes of the slice: x: 2, y: 2, z: 4, core: 2. Of those that a mesh axis runs over, the one named last changes fastest.
Arguments:
- hidden_in: bfloat16 [8192, 768], P(('dp', 'tensor')), may hold values from -40 to 40
- segment_ids: int32 [16, 512], P('dp'), may hold values from 0 to 7, never falling along the last dimension, each value on 1 to 256 neighbouring positions
- cotangent: float32 [8192, 768], P(('dp', 'tensor')), may hold values from -6 to 6
- norm1_gain: float32 [768], P(('dp', 'tensor')), may hold values from 0.5 to 1.5
- norm1_bias: float32 [768], P(('dp', 'tensor')), may hold values from -2 to 2
- norm2_gain: float32 [768], P(('dp', 'tensor')), may hold values from 0.5 to 1.5
- norm2_bias: float32 [768], P(('dp', 'tensor')), may hold values from -2 to 2
- qkv_weight: bfloat16 [768, 2304], P('dp', 'tensor'), may hold values from -2 to 2
- qkv_bias: bfloat16 [12, 192], P('tensor', 'dp'), may hold values from -3 to 3
- dense_weight: bfloat16 [768, 768], P('tensor', 'dp'), may hold values from -0.875 to 0.875
- dense_bias: float32 [768], P(('dp', 'tensor')), may hold values from -3 to 3
- up_weight: bfloat16 [768, 3072], P('dp', 'tensor'), may hold values from -0.21875 to 0.21875
- up_bias: bfloat16 [12, 256], P('tensor', 'dp'), may hold values from -3 to 3
- down_weight: bfloat16 [3072, 768], P('tensor', 'dp'), may hold values from -0.109375 to 0.109375
- down_bias: float32 [768], P(('dp', 'tensor')), may hold values from -3 to 3
Outputs:
- hidden_out: float32 [8192, 768], P(('dp', 'tensor'))
- hidden_grad: float32 [8192, 768], P(('dp', 'tensor'))
- norm1_gain_grad: float32 [768], P(('dp', 'tensor'))
- norm1_bias_grad: float32 [768], P(('dp', 'tensor'))
- norm2_gain_grad: float32 [768], P(('dp', 'tensor'))
- norm2_bias_grad: float32 [768], P(('dp', 'tensor'))
- qkv_weight_grad: float32 [768, 2304], P('dp', 'tensor')
- qkv_bias_grad: float32 [12, 192], P('tensor', 'dp')
- dense_weight_grad: float32 [768, 768], P('tensor', 'dp')
- dense_bias_grad: float32 [768], P(('dp', 'tensor'))
- up_weight_grad: float32 [768, 3072], P('dp', 'tensor')
- up_bias_grad: float32 [12, 256], P('tensor', 'dp')
- down_weight_grad: float32 [3072, 768], P('tensor', 'dp')
- down_bias_grad: float32 [768], P(('dp', 'tensor'))
Inputs may be any that keep to these rules, and one draw needn't show every extreme that they name: `segment_ids`: within each row of 512 tokens the ids never fall; each document holds 1 to 256 tokens, and some document holds exactly 256.
All inputs are finite; a program needn't handle non-finite values.
Results may differ from a plain program's by a relative error of at most 0.0082.
Values may be sent and summed in bfloat16 or wider, within the bound.
No kernel may reach another device: no remote copies, remote signals or barrier semaphores. Data moves between devices by JAX's collectives and lax.ppermute only.
A program may use at most 128 MiB of HBM per device.

v0:
```python
import functools
import math

import jax
import jax.numpy as jnp
from jax import lax
from jax.experimental import pallas as pl
from jax.experimental.pallas import tpu as pltpu
from jax.sharding import PartitionSpec as P


HD = 64
ROT = 16
MAX_DOC = 256
QB = 128
norm_eps = 1e-05

BF = jnp.bfloat16
F32 = jnp.float32


def dot(a, b):
    return lax.dot_general(a, b, (((1,), (0,)), ((), ())), preferred_element_type=F32)


def dot_t(a, b):
    return lax.dot_general(a, b, (((1,), (1,)), ((), ())), preferred_element_type=F32)


def t_dot(a, b):
    return lax.dot_general(a, b, (((0,), (0,)), ((), ())), preferred_element_type=F32)


def vmem(mib):
    return pltpu.CompilerParams(vmem_limit_bytes=mib * 1024 * 1024)


def cost(flops, ins, outs):
    size = sum(a.size * a.dtype.itemsize for a in (*ins, *outs))
    return pl.CostEstimate(flops=int(flops), bytes_accessed=int(size), transcendentals=0)


def whole(shape):
    zeros = (0,) * len(shape)
    return pl.BlockSpec(tuple(shape), lambda i, *_: zeros)


def swap(array, axis, size, bits):
    return lax.ppermute(array, axis, [(i, i ^ bits) for i in range(size)])


def rotate(wide, tables, sign):
    width = wide.shape[-1]
    half = ROT // 2
    lane = lax.broadcasted_iota(jnp.int32, (1, width), 1)
    turns = ((lane // HD) % 3 < 2).astype(F32)
    reps = width // tables.shape[-1]
    cosine, low, high = (jnp.concatenate([tables[j]] * reps, axis=1) * turns for j in range(3))
    down = pltpu.roll(wide, width - half, 1)
    up = pltpu.roll(wide, half, 1)
    return wide + wide * cosine + sign * (down * low + up * high)


EXCHANGE = (0, 2, 4, 6, 1, 3, 5, 7)
SMALL_ROWS = 16
SMALL_LANES = 128


def assemble_body(place, *refs, count, rows, small):
    blocks = refs[:count]
    full = refs[count]
    sems = refs[-1]
    copies = []
    for at, k in enumerate(EXCHANGE):
        start = pl.multiple_of((place[0] ^ k) * rows, 16)
        copies.append(
            pltpu.make_async_copy(
                blocks[at].at[pl.ds(0, rows), :], full.at[pl.ds(start, rows), :], sems.at[at]
            )
        )
        if small:
            copies.append(
                pltpu.make_async_copy(
                    blocks[at].at[pl.ds(rows, SMALL_ROWS), :], refs[-2].at[place[0] ^ k], sems.at[count + at]
                )
            )
    for copy in copies:
        copy.start()
    for copy in copies:
        copy.wait()
    if small:
        gains, qb, ub = refs[count + 1 : count + 4]
        nvec, heads, units = small
        lanes = SMALL_LANES
        qpart, upart = qb.shape[1] // heads // count, ub.shape[1] // units // count
        for d in range(count):
            wide = refs[-2][d].astype(F32)
            vals = wide[:, :lanes] + wide[:, lanes : 2 * lanes] + wide[:, 2 * lanes : 3 * lanes]
            gains[0:nvec, d * rows : (d + 1) * rows] = vals[0:nvec, :rows]
            for h in range(heads):
                at = (h * count + d) * qpart
                qb[:, at : at + qpart] = vals[nvec + h : nvec + h + 1, :qpart]
            for u in range(units):
                at = (u * count + d) * upart
                row = nvec + heads + u
                ub[:, at : at + upart] = vals[row : row + 1, :upart]


def assemble(place, blocks, rows, small):
    count = len(blocks)
    cols = blocks[0].shape[1]
    anywhere = pl.BlockSpec(memory_space=pl.ANY)
    outs = [jax.ShapeDtypeStruct((count * rows, cols), BF)]
    specs = [anywhere]
    scratch = []
    if small:
        nvec, qcols, heads, fcols, units = small
        outs += [
            jax.ShapeDtypeStruct(shape, F32) for shape in ((nvec, count * rows), (1, qcols), (1, fcols))
        ]
        specs += [whole(o.shape) for o in outs[1:]]
        scratch = [pltpu.VMEM((count, SMALL_ROWS, cols), BF)]
        small = (nvec, heads, units)
    return pl.pallas_call(
        functools.partial(assemble_body, count=count, rows=rows, small=small),
        grid_spec=pltpu.PrefetchScalarGridSpec(
            num_scalar_prefetch=1,
            grid=(1,),
            in_specs=[anywhere] * count,
            out_specs=specs,
            scratch_shapes=scratch + [pltpu.SemaphoreType.DMA((2 * count,))],
        ),
        out_shape=outs,
        compiler_params=vmem(4),
    )(place, *blocks)


def prep_body(meta, cot, half_o, sum_o):
    half_o[...] = cot[...].astype(BF)
    sum_o[...] = jnp.broadcast_to(jnp.sum(cot[...], axis=0, keepdims=True), sum_o.shape)


def final_body(meta, own, one, two, hid, cot, out_o):
    x = hid[...].astype(F32)
    cent = x - jnp.mean(x, axis=-1, keepdims=True)
    inverse = lax.rsqrt(jnp.mean(cent * cent, axis=-1, keepdims=True) + norm_eps)
    normed = cent * inverse
    n = own[...].astype(F32) + one[...].astype(F32) + two[...].astype(F32)
    out_o[...] = cot[...] + inverse * (
        n - jnp.mean(n, axis=-1, keepdims=True) - normed * jnp.mean(n * normed, axis=-1, keepdims=True)
    )


def windows(length):
    reach = -(-(MAX_DOC - 1) // QB)
    return [(max(0, i - reach) * QB, (i + 1) * QB) for i in range(length // QB)]


def spot(meta, a, tokens):
    return pl.ds(pl.multiple_of(((meta[0] % 2) ^ a) * tokens, tokens), tokens)


def attn_fwd_body(
    meta, hid_a, hid_b, gains, wa, qb, tables, segc, segr,
    xhat_o, first_o, second_o, mixed_o, att_o, p_o, scratch,
):
    qcols = qb.shape[1]
    tokens = hid_a.shape[0]
    for a, hid in enumerate((hid_a, hid_b)):
        at = spot(meta, a, tokens)
        x = hid[...].astype(F32)
        cent = x - jnp.mean(x, axis=-1, keepdims=True)
        spread = jnp.mean(cent * cent, axis=-1, keepdims=True)
        xhat = cent * lax.rsqrt(spread + norm_eps)
        xhat_o[at, :] = xhat.astype(BF)
        first_o[at, :] = (xhat * gains[0:1, :] + gains[1:2, :]).astype(BF)
        second_o[at, :] = (xhat * gains[2:3, :] + gains[3:4, :]).astype(BF)
    seqs, _, length = segr.shape
    heads = qcols // (3 * HD)
    scratch[...] = jnp.zeros_like(scratch)
    for r in range(seqs):
        row = slice(r * length, (r + 1) * length)
        scratch[:, :qcols] = dot(first_o[row, :], wa[:, :qcols]) + qb[...]
        mixed_o[row, :] = rotate(scratch[...], tables, 1.0).astype(BF)
    for r in range(seqs):
        start = r * length
        for i, (lo, hi) in enumerate(windows(length)):
            width = hi - lo
            qs = slice(start + i * QB, start + (i + 1) * QB)
            ks = slice(start + lo, start + hi)
            rows = lax.broadcasted_iota(jnp.int32, (QB, width), 0) + i * QB
            cols = lax.broadcasted_iota(jnp.int32, (QB, width), 1) + lo
            mask = (segc[qs, :] == segr[r, :, lo:hi]) & (rows >= cols)
            for h in range(heads):
                base = h * 3 * HD
                q = mixed_o[qs, base : base + HD]
                k = mixed_o[ks, base + HD : base + 2 * HD]
                v = mixed_o[ks, base + 2 * HD : base + 3 * HD]
                s = jnp.where(mask, dot_t(q, k) * (HD**-0.5), -1e30)
                p = jnp.exp(s - jnp.max(s, axis=-1, keepdims=True))
                w = (p * (1.0 / jnp.sum(p, axis=-1, keepdims=True))).astype(BF)
                att_o[qs, h * HD : (h + 1) * HD] = dot(w, v).astype(BF)
                p_o[r, h, i, :, :width] = w


def mlp_fwd_body(meta, second, att, wa, wb, ub, active_o, slope_o, out_a, out_b, both, *, qcols):
    fcols = ub.shape[1]
    tokens = out_a.shape[0]

    @pl.loop(0, 2)
    def _(i):
        at = pl.ds(pl.multiple_of(i * tokens, tokens), tokens)
        pre = dot(second[at, :], wb[:, :fcols]) + ub[...]
        cumulative = 0.5 * (1.0 + lax.erf(pre * (1.0 / math.sqrt(2.0))))
        density = jnp.exp(-0.5 * pre * pre) * (1.0 / math.sqrt(2.0 * math.pi))
        act = (pre * cumulative).astype(BF)
        active_o[at, :] = act
        slope_o[at, :] = (cumulative + pre * density).astype(BF)
        both[at, :] = (dot_t(att[at, :], wa[:, qcols:]) + dot_t(act, wb[:, fcols:])).astype(BF)

    out_a[...] = both[spot(meta, 0, tokens), :]
    out_b[...] = both[spot(meta, 1, tokens), :]


def mlp_bwd_body(
    meta, cot_a, cot_b, act, slope, second, xhat, gains, wb, *refs, fcols, blocks, split, chained,
):
    tokens = cot_a.shape[0]
    if chained:
        up_in, down_in, ub_in, stat_in, n_o, keep_o, send_o, ub_o, stat_o, gup, gdown = refs
    else:
        n_o, gup, gdown, ub_o, stat_o = refs
    for a, ref in enumerate((cot_a, cot_b)):
        at = spot(meta, a, tokens)
        c = ref[...]
        down = t_dot(c, act[at, :])
        gp = dot(c, wb[:, fcols:]) * slope[at, :].astype(F32)
        gph = gp.astype(BF)
        up = t_dot(second[at, :], gph)
        part = dot_t(gph, wb[:, :fcols])
        n_o[at, :] = (part * gains[2:3, :]).astype(BF)
        sums = (
            jnp.sum(gp, axis=0, keepdims=True),
            jnp.sum(part * xhat[at, :].astype(F32), axis=0, keepdims=True),
            jnp.sum(part, axis=0, keepdims=True),
        )
        if a:
            gdown[...] += down
            gup[...] += up
            ub_o[0:1, :] += sums[0]
            stat_o[0:1, :] += sums[1]
            stat_o[1:2, :] += sums[2]
        elif chained:
            gdown[...] = down_in[...] + down
            gup[...] = up_in[...] + up
            ub_o[0:1, :] = ub_in[0:1, :] + sums[0]
            stat_o[0:1, :] = stat_in[0:1, :] + sums[1]
            stat_o[1:2, :] = stat_in[1:2, :] + sums[2]
        else:
            gdown[...] = down
            gup[...] = up
            ub_o[0:1, :] = sums[0]
            stat_o[0:1, :] = sums[1]
            stat_o[1:2, :] = sums[2]
    if chained:
        emit(meta, (gup, gdown), keep_o, send_o, blocks, split)


def emit(meta, parts, keep_o, send_o, blocks, split):
    rows = keep_o.shape[1]
    for k in range(blocks):
        if split:
            start = pl.multiple_of((meta[1] ^ k) * rows, 16)
            target = send_o if k % 2 else keep_o
            slot = k // 2
        else:
            start, target, slot = k * rows, keep_o, k
        at = 0
        for part in parts:
            wide = part.shape[1]
            target[slot, :, at : at + wide] = part[pl.ds(start, rows), :].astype(target.dtype)
            at += wide


def attn_bwd_body(
    meta, cot_a, cot_b, mix, p_in, att, first, xhat, n_in, gains, wa, tables,
    n_a, n_b, stat_o, qb_o, gqkv, gdense, dmix, cot, *, heads, qcols, seqs, last,
):
    tokens = cot_a.shape[0]
    for a, ref in enumerate((cot_a, cot_b)):
        cot[spot(meta, a, tokens), :] = ref[...]
    c = cot[...]
    length = c.shape[0] // seqs
    down = t_dot(c, att[...])
    gdense[...] = down if last is None else last[1][...] + down
    ga = dot(c, wa[:, qcols:]).astype(BF)
    dmix[...] = jnp.zeros_like(dmix)
    for r in range(seqs):
        start = r * length
        for h in range(heads):
            base = h * 3 * HD
            for i, (lo, hi) in enumerate(windows(length)):
                width = hi - lo
                qs = slice(start + i * QB, start + (i + 1) * QB)
                ks = slice(start + lo, start + hi)
                q = mix[qs, base : base + HD]
                k = mix[ks, base + HD : base + 2 * HD]
                v = mix[ks, base + 2 * HD : base + 3 * HD]
                g = ga[qs, h * HD : (h + 1) * HD]
                w = p_in[r, h, i, :, :width]
                wide = w.astype(F32)
                gw = dot_t(g, v)
                inner = jnp.sum(wide * gw, axis=-1, keepdims=True)
                ds = (wide * (gw - inner) * (HD**-0.5)).astype(BF)
                dmix[qs, base : base + HD] = dot(ds, k)
                dmix[ks, base + HD : base + 2 * HD] += t_dot(ds, q)
                dmix[ks, base + 2 * HD : base + 3 * HD] += t_dot(w, g)
        row = slice(start, start + length)
        dmix[row, :] = rotate(dmix[row, :], tables, -1.0)
    turned = dmix[...]
    total = jnp.sum(turned, axis=0, keepdims=True)
    qb_o[0:1, :] = total if last is None else last[3][0:1, :] + total
    g = turned[:, :qcols].astype(BF)
    up = t_dot(first[...], g)
    gqkv[...] = up if last is None else last[0][...] + up
    part = dot_t(g, wa[:, :qcols])
    sums = (
        jnp.sum(part * xhat[...].astype(F32), axis=0, keepdims=True),
        jnp.sum(part, axis=0, keepdims=True),
    )
    for j in range(2):
        stat_o[j : j + 1, :] = sums[j] if last is None else last[2][j : j + 1, :] + sums[j]
    cot[...] = (part * gains[0:1, :] + n_in[...].astype(F32)).astype(BF)
    for a, out in enumerate((n_a, n_b)):
        out[...] = cot[spot(meta, a, tokens), :]


def pack_body(
    meta, gqkv, gdense, stat, stat_two, cot_sum, ub, qb, keep_o, send_o, wide, cols,
    *, blocks, split, heads, units,
):
    rows = keep_o.shape[1]
    lanes = cols.shape[1]
    wide[...] = jnp.zeros_like(wide)
    wide[0:2, :] = stat[0:2, :]
    wide[2:4, :] = stat_two[0:2, :]
    wide[4:5, :] = cot_sum[0:1, :]
    cols[...] = wide[...].T
    for lane_at, source, groups, size in ((5, ub, units, ub.shape[1] // units), (7, qb, heads, 3 * HD)):
        per = size // blocks
        tall = jnp.broadcast_to(source[0:1, :], (lanes, source.shape[1])).T
        lane = lax.broadcasted_iota(jnp.int32, (per, lanes), 1)
        for d in range(blocks):
            for g in range(groups):
                at = slice(d * rows + g * per, d * rows + (g + 1) * per)
                src = tall[g * size + d * per : g * size + (d + 1) * per, :]
                cols[at, :] = jnp.where(lane == lane_at, src, cols[at, :])
    emit(meta, (gqkv, gdense, cols), keep_o, send_o, blocks, split)


def gather_weights(shard, rows, place, dp, small=None):
    got = {k: swap(shard, "dp", dp, k) for k in (6, 2, 4)}
    near = [shard] + [got[k] for k in (2, 4, 6)]
    far = [swap(a, "dp", dp, 1) for a in near]
    return assemble(place, near + far, rows, small)


def reduce_weights(keep, send, dp):
    if send is None:
        total = lax.psum_scatter(keep, "dp", scatter_dimension=0, tiled=True)
        return total[0]
    got = swap(send, "dp", dp, 1)
    near = [keep[j].astype(F32) + got[j].astype(F32) for j in range(keep.shape[0])]
    total = near[0]
    for j in (3, 1, 2):
        total = total + swap(near[j].astype(BF), "dp", dp, 2 * j).astype(F32)
    return total


def rotary_tables(length):
    place = jnp.arange(length).astype(F32)[:, None]
    entry = jnp.arange(128) % HD
    half = ROT // 2
    turns = (entry < ROT)[None, :]
    frequency = 1.0 / 10000.0 ** ((entry % half).astype(F32) * 2.0 / ROT)
    angle = place * frequency[None, :]
    cosine = jnp.where(turns, jnp.cos(angle) - 1.0, 0.0)
    sine = jnp.where(turns, jnp.sin(angle), 0.0)
    low = (entry < half)[None, :]
    return jnp.stack([cosine, jnp.where(low, -sine, 0.0), jnp.where(low, 0.0, sine)])


def call(body, out_shape, scratch, *args, mib=16, flops=0):
    return pl.pallas_call(
        body,
        grid_spec=pltpu.PrefetchScalarGridSpec(
            num_scalar_prefetch=1,
            grid=(1,),
            in_specs=[whole(a.shape) for a in args[1:]],
            out_specs=[whole(o.shape) for o in out_shape],
            scratch_shapes=[pltpu.VMEM(shape, dtype) for shape, dtype in scratch],
        ),
        out_shape=out_shape,
        compiler_params=vmem(mib),
        cost_estimate=cost(flops, args[1:], out_shape),
    )(*args)


def block(
    hidden_in, segment_ids, cotangent, norm1_gain, norm1_bias, norm2_gain, norm2_bias,
    qkv_weight, qkv_bias, dense_weight, dense_bias, up_weight, up_bias, down_weight, down_bias,
    *, dp, tensor,
):
    d_at = lax.axis_index("dp")
    z_at = lax.axis_index("tensor")
    meta = jnp.stack([z_at, d_at]).astype(jnp.int32)
    place = d_at.astype(jnp.int32)[None]
    tokens, width = hidden_in.shape
    seqs, length = segment_ids.shape
    hseqs = seqs // 2
    htok = tokens * tensor // 2
    qcols = qkv_weight.shape[1]
    heads = qcols // (3 * HD)
    acols = heads * HD
    fcols = up_weight.shape[1]
    qwide = -(-qcols // 128) * 128
    rows = width // dp
    split = dp == len(EXCHANGE) and rows % 16 == 0
    stat_lanes = 128

    def sds(shape, dtype=F32):
        return jax.ShapeDtypeStruct(shape, dtype)

    def zswap(a, bits):
        return swap(a, "tensor", tensor, bits)

    vecs = jnp.stack([norm1_gain, norm1_bias, norm2_gain, norm2_bias, dense_bias, down_bias])
    nvec, part = vecs.shape
    got = [vecs] + [zswap(vecs, k) for k in range(1, tensor)]
    lanes_of = []
    for t in range(tensor):
        value = got[0]
        for k in range(1, tensor):
            value = jnp.where(z_at == t ^ k, got[k], value)
        lanes_of.append(value)
    units = up_bias.shape[0]

    def lanes(a):
        return jnp.pad(a.astype(F32), ((0, 0), (0, SMALL_LANES - a.shape[1])))

    small = jnp.concatenate(
        [
            lanes(jnp.concatenate(lanes_of, axis=1)), lanes(qkv_bias), lanes(up_bias),
            jnp.zeros((SMALL_ROWS - nvec - heads - units, SMALL_LANES), F32),
        ],
        axis=0,
    )
    high = lax.reduce_precision(small, 8, 7)
    middle = lax.reduce_precision(small - high, 8, 7)
    low = small - high - middle
    triple = jnp.concatenate([high, middle, low], axis=1).astype(BF)

    half_cot, cot_sum = call(prep_body, [sds((tokens, width), BF), sds((8, width))], [], meta, cotangent, mib=4)
    hid_two = zswap(hidden_in, 2)
    hid_one = zswap(hidden_in, 1)
    hid_three = zswap(hid_two, 1)
    cot_two = zswap(half_cot, 2)
    cot_one = zswap(half_cot, 1)
    cot_three = zswap(cot_two, 1)

    acols_all = qcols + acols
    triple = jnp.pad(triple, ((0, 0), (0, acols_all - triple.shape[1])))
    pack_a = jnp.concatenate(
        [jnp.concatenate([qkv_weight, dense_weight.T], axis=1), triple], axis=0
    )
    pack_b = jnp.concatenate([up_weight, down_weight.T], axis=1)
    if split:
        wa, gains, qb, ub = gather_weights(pack_a, rows, place, dp, (nvec, qcols, heads, fcols, units))
        (wb,) = gather_weights(pack_b, rows, place, dp)
    else:
        every = lax.all_gather(pack_a, "dp", axis=0)
        wa = every[:, :rows].reshape(width, acols_all)
        wb = lax.all_gather(pack_b, "dp", axis=0, tiled=True)
        trio = every[:, rows:].astype(F32)
        vals = sum(trio[:, :, j * SMALL_LANES : (j + 1) * SMALL_LANES] for j in range(3))
        gains = vals[:, :nvec, :rows].transpose(1, 0, 2).reshape(nvec, width)
        qb = vals[:, nvec : nvec + heads, : 3 * HD // dp].transpose(1, 0, 2).reshape(1, qcols)
        ub = vals[:, nvec + heads : nvec + heads + units, : fcols // units // dp]
        ub = ub.transpose(1, 0, 2).reshape(1, fcols)
    tables = rotary_tables(length)

    side = z_at // 2
    near_ids = lax.dynamic_slice_in_dim(segment_ids, side * hseqs, hseqs, 0)
    far_ids = lax.dynamic_slice_in_dim(segment_ids, (1 - side) * hseqs, hseqs, 0)
    nwin = length // QB
    wwin = max(hi - lo for lo, hi in windows(length))

    def forward(hid_a, hid_b, ids):
        fa = call(
            attn_fwd_body,
            [
                sds((htok, width), BF), sds((htok, width), BF), sds((htok, width), BF),
                sds((htok, qwide), BF), sds((htok, acols), BF), sds((hseqs, heads, nwin, QB, wwin), BF),
            ],
            [((htok, qwide), F32)],
            meta, hid_a, hid_b, gains, wa, qb, tables, ids.reshape(htok, 1),
            ids.reshape(hseqs, 1, length), flops=7e9,
        )
        xhat, first, second, mixed, att, weights = fa
        active, slope, out_a, out_b = call(
            functools.partial(mlp_fwd_body, qcols=qcols),
            [
                sds((htok, fcols), BF), sds((htok, fcols), BF), sds((tokens, width), BF),
                sds((tokens, width), BF),
            ],
            [((htok, width), BF)], meta, second, att, wa, wb, ub, flops=3e9,
        )
        return dict(
            xhat=xhat, first=first, second=second, mixed=mixed, att=att, weights=weights,
            active=active, slope=slope, out=(out_a, out_b),
        )

    near = forward(hidden_in, hid_one, near_ids)
    far = forward(hid_two, hid_three, far_ids)

    def scatter(near_parts, far_parts):
        relay = zswap(far_parts[1], 1)
        pair = (far_parts[0].astype(F32) + relay.astype(F32)).astype(BF)
        two = zswap(pair, 2)
        one = zswap(near_parts[1], 1)
        return near_parts[0], one, two

    branch = sum(a.astype(F32) for a in scatter(near["out"], far["out"]))
    hidden_out = hidden_in.astype(F32) + branch + gains[4] + gains[5]

    if split:
        half_blocks = (dp // 2, rows)
    else:
        half_blocks = (dp, rows)

    def grad_shapes(cols):
        return [sds(half_blocks + (cols,)), sds(half_blocks + (cols,) if split else (1, 16, 128), BF)]

    def mlp_bwd(cot_a, cot_b, kept, before):
        sums = [sds((8, fcols)), sds((8, width))]
        grads = [sds((width, fcols)), sds((width, fcols))]
        chained = before is not None
        return call(
            functools.partial(mlp_bwd_body, fcols=fcols, blocks=dp, split=split, chained=chained),
            [sds((htok, width), BF)] + (grad_shapes(2 * fcols) + sums if chained else grads + sums),
            [((width, fcols), F32)] * 2 if chained else [],
            meta, cot_a, cot_b, *(kept[k] for k in ("active", "slope", "second", "xhat")), gains, wb,
            *(before if chained else ()), flops=5e9,
        )

    n_two_far, *sums_far = mlp_bwd(cot_two, cot_three, far, None)
    n_two_near, b_keep, b_send, ub_sum, stat_two = mlp_bwd(half_cot, cot_one, near, sums_far)

    def attn_bwd(cot_a, cot_b, kept, n_half, before):
        fixed = 12

        def body(*refs):
            ins = refs[:fixed]
            last = None if before is None else (refs[fixed], refs[fixed + 1], refs[fixed + 2], refs[fixed + 3])
            outs = refs[fixed + (0 if before is None else 4) :]
            attn_bwd_body(*ins, *outs, heads=heads, qcols=qcols, seqs=hseqs, last=last)

        return call(
            body,
            [
                sds((tokens, width), BF), sds((tokens, width), BF), sds((8, width)), sds((8, qwide)),
                sds((width, qcols)), sds((width, acols)),
            ],
            [((htok, qwide), F32), ((htok, width), BF)],
            meta, cot_a, cot_b, kept["mixed"], kept["weights"], kept["att"], kept["first"], kept["xhat"],
            n_half, gains, wa, tables, *(() if before is None else before), flops=9e9,
        )

    *n_far, s_far, q_far, gqkv_far, gdense_far = attn_bwd(cot_two, cot_three, far, n_two_far, None)
    *n_near, stat_one, qb_sum, gqkv, gdense = attn_bwd(
        half_cot, cot_one, near, n_two_near, (gqkv_far, gdense_far, s_far, q_far)
    )
    a_keep, a_send = call(
        functools.partial(pack_body, blocks=dp, split=split, heads=heads, units=units),
        grad_shapes(qcols + acols + stat_lanes),
        [((stat_lanes, width), F32), ((width, stat_lanes), F32)],
        meta, gqkv, gdense, stat_one, stat_two, cot_sum, ub_sum, qb_sum, flops=1e9,
    )

    b_grad = reduce_weights(b_keep, b_send if split else None, dp)
    grad_parts = scatter(n_near, n_far)
    a_grad = reduce_weights(a_keep, a_send if split else None, dp)
    (hidden_grad,) = call(
        final_body, [sds((tokens, width))], [], meta, *grad_parts, hidden_in, cotangent, mib=8, flops=2e9
    )

    stats = a_grad[:, qcols + acols :]
    qb_grad = stats[: heads * (3 * HD // dp), 7].reshape(heads, -1)
    ub_grad = stats[: fcols // dp, 5].reshape(up_bias.shape[0], -1)
    total = stats
    for k in range(1, tensor):
        total = total + zswap(stats, k)
    mine = lax.dynamic_slice_in_dim(total, z_at * part, part, 0)[:, :8].T

    return (
        hidden_out,
        hidden_grad,
        mine[0],
        mine[1],
        mine[2],
        mine[3],
        a_grad[:, :qcols],
        qb_grad,
        a_grad[:, qcols : qcols + acols].T,
        mine[4],
        b_grad[:, :fcols],
        ub_grad,
        b_grad[:, fcols:].T,
        mine[4],
    )


def solution(mesh):
    both = P(("dp", "tensor"))
    wide = P(("dp", "tensor"), None)
    step = jax.shard_map(
        functools.partial(block, dp=mesh.shape["dp"], tensor=mesh.shape["tensor"]),
        mesh=mesh,
        in_specs=(
            wide, P("dp", None), wide, both, both, both, both, P("dp", "tensor"),
            P("tensor", "dp"), P("tensor", "dp"), both, P("dp", "tensor"), P("tensor", "dp"),
            P("tensor", "dp"), both,
        ),
        out_specs=(
            wide, wide, both, both, both, both, P("dp", "tensor"), P("tensor", "dp"),
            P("tensor", "dp"), both, P("dp", "tensor"), P("tensor", "dp"), P("tensor", "dp"), both,
        ),
        check_vma=False,
    )
    if mesh.shape["dp"] != len(EXCHANGE):
        return step
    return step
```

profile of v0, /device:TPU:0, one launch (start us, length us, event | category | flops | bytes accessed | tf_op | source)
XLA Modules:
  0.0 191.2 jit_solution(2328525761547804958)
XLA Ops:
  1.5 3.1 %collective-permute-start.3 = (f32[6,24]{1,0:T(8,128)S(1)}, f32[6,24]{1,0:T(8,128)S(1)}, u32[]{:S(2)}, u32[]{:S(2)}) collective-permute-start(f32[6,24]{1,0:T(8,128)S(1)} %stack.45), channel_id=1, source_target_pairs={{0,1},{1,0},{2,3},{3,2},{4,5},{5,4},{6,7},{7,6},{8,9},{9,8},{10,11... | collective-permute-start | bytes 1736 | tf_op jit(solution)/shard_map/ppermute | solution.py:49
  4.6 2.6 %collective-permute-start.2 = (f32[6,24]{1,0:T(8,128)S(1)}, f32[6,24]{1,0:T(8,128)S(1)}, u32[]{:S(2)}, u32[]{:S(2)}) collective-permute-start(f32[6,24]{1,0:T(8,128)S(1)} %stack.45), channel_id=1, source_target_pairs={{0,2},{1,3},{2,0},{3,1},{4,6},{5,7},{6,4},{7,5},{8,10},{9,11},{10,... | collective-permute-start | bytes 1736 | tf_op jit(solution)/shard_map/ppermute | solution.py:49
  10.8 1.8 collective-permute-done.1
  13.8 2.5 %collective-permute-start.6 = (bf16[112,768]{1,0:T(8,128)(2,1)S(1)}, bf16[112,768]{1,0:T(8,128)(2,1)S(1)}, u32[]{:S(2)}, u32[]{:S(2)}) collective-permute-start(bf16[112,768]{1,0:T(8,128)(2,1)S(1)} %pad_maximum_fusion.2.refs_0_), channel_id=1, source_target_pairs={{0,24},{4,28},{8,16},{12,20},{16,8},{20,12},{24,0},{28,4},{1,25},{... | collective-permute-start | bytes 516104 | tf_op jit(solution)/shard_map/ppermute | solution.py:49
  17.3 4.3 %collective-permute-done.6.refs_3_ = bf16[112,768]{1,0:T(8,128)(2,1)S(1)} collective-permute-done((bf16[112,768]{1,0:T(8,128)(2,1)S(1)}, bf16[112,768]{1,0:T(8,128)(2,1)S(1)}, u32[]{:S(2)}, u32[]{:S(2)}) %collective-permute-start.6) | collective-permute-done | bytes 172064 | tf_op jit(solution)/shard_map/ppermute | solution.py:49
  21.6 1.8 collective-permute-done.5.refs_2_
  24.8 3.5 %collective-permute-start.19 = (bf16[256,768]{1,0:T(8,128)(2,1)}, bf16[256,768]{1,0:T(8,128)(2,1)}, u32[]{:S(2)}, u32[]{:S(2)}) collective-permute-start(bf16[256,768]{1,0:T(8,128)(2,1)} %hid.1), channel_id=1, source_target_pairs={{0,2},{1,3},{2,0},{3,1},{4,6},{5,7},{6,4},{7,5},{8,10},{9,11},{10,... | collective-permute-start | bytes 1179656 | tf_op jit(solution)/shard_map/ppermute | solution.py:49
  29.4 1.8 collective-permute-start.13
  31.2 1.2 collective-permute-start.12
  34.9 2.6 %shard_map.254 = (bf16[768,768]{1,0:T(8,128)(2,1)S(1)}, f32[6,768]{1,0:T(8,128)S(1)}, f32[1,576]{1,0:T(1,128)S(1)}, f32[1,768]{1,0:T(1,128)S(1)}) custom-call(s32[1]{0:T(128)} %bitcast.1.place, bf16[112,768]{1,0:T(8,128)(2,1)S(1)} %pad_maximum_fusion.2.refs_0_, bf16[112,768]{1,0:T(8,128)(2,1)S(1)} %collective-permute-done.4.refs_1_, ...), custom_call_target="tpu_custom_call" | custom-call | tf_op jit(solution)/shard_map/pallas_call | solution.py:124
  37.5 2.7 %collective-permute-done.13.refs_3_ = bf16[96,1536]{1,0:T(8,128)(2,1)S(1)} collective-permute-done((bf16[96,1536]{1,0:T(8,128)(2,1)S(1)}, bf16[96,1536]{1,0:T(8,128)(2,1)S(1)}, u32[]{:S(2)}, u32[]{:S(2)}) %collective-permute-start.13) | collective-permute-done | bytes 294944 | tf_op jit(solution)/shard_map/ppermute | solution.py:49
  40.3 4.8 %collective-permute-done.12.refs_2_ = bf16[96,1536]{1,0:T(8,128)(2,1)S(1)} collective-permute-done((bf16[96,1536]{1,0:T(8,128)(2,1)S(1)}, bf16[96,1536]{1,0:T(8,128)(2,1)S(1)}, u32[]{:S(2)}, u32[]{:S(2)}) %collective-permute-start.12) | collective-permute-done | bytes 294944 | tf_op jit(solution)/shard_map/ppermute | solution.py:49
  45.7 9.2 %collective-permute-done.19.hid_a = bf16[256,768]{1,0:T(8,128)(2,1)} collective-permute-done((bf16[256,768]{1,0:T(8,128)(2,1)}, bf16[256,768]{1,0:T(8,128)(2,1)}, u32[]{:S(2)}, u32[]{:S(2)}) %collective-permute-start.19) | collective-permute-done | bytes 393248 | tf_op jit(solution)/shard_map/ppermute | solution.py:49
  55.1 7.8 %shard_map.255 = (bf16[512,768]{1,0:T(8,128)(2,1)S(1)}, bf16[512,768]{1,0:T(8,128)(2,1)S(1)}, bf16[512,768]{1,0:T(8,128)(2,1)S(1)}, bf16[512,640]{1,0:T(8,128)(2...) custom-call(s32[2]{0:T(128)S(1)} %pad_add_fusion.meta.refs_0_, ...), custom_call_target="tpu_custom_call" | custom-call | flops 7000000000 | bytes 7168256 | tf_op jit(solution)/shard_map/pallas_call | solution.py:394
  63.1 1.8 collective-permute-start.23
  65.8 3.0 %shard_map.257 = (bf16[512,768]{1,0:T(8,128)(2,1)S(1)}, bf16[512,768]{1,0:T(8,128)(2,1)S(1)}, bf16[256,768]{1,0:T(8,128)(2,1)S(1)}, bf16[256,768]{1,0:T(8,128)(2,1)S(1)}) custom-call(s32[2]{0:T(128)S(1)} %pad_add_fusion.meta.refs_0_, bf16[512,768]{1,0:T(8,128)(2,1)S(1)} %get-tuple-element.67.second, bf16[512,192]{1,0:T(8,128)(2,1)S(1)} %get-tuple-element.68.att.refs_5_, ...), custom_call_target="tpu_custom_call" | custom-call | flops 3000000000 | bytes 6884352 | tf_op jit(solution)/shard_map/pallas_call | solution.py:394
  69.6 1.9 %collective-permute-done.20.hid_b = bf16[256,768]{1,0:T(8,128)(2,1)S(1)} collective-permute-done((bf16[256,768]{1,0:T(8,128)(2,1)}, bf16[256,768]{1,0:T(8,128)(2,1)S(1)}, u32[]{:S(2)}, u32[]{:S(2)}) %collective-permute-start.20) | collective-permute-done | bytes 393248 | tf_op jit(solution)/shard_map/ppermute | solution.py:49
  71.5 7.8 %shard_map.258 = (bf16[512,768]{1,0:T(8,128)(2,1)S(1)}, bf16[512,768]{1,0:T(8,128)(2,1)S(1)}, bf16[512,768]{1,0:T(8,128)(2,1)S(1)}, bf16[512,640]{1,0:T(8,128)(2...) custom-call(s32[2]{0:T(128)S(1)} %pad_add_fusion.meta.refs_0_, ...), custom_call_target="tpu_custom_call" | custom-call | flops 7000000000 | bytes 7168256 | tf_op jit(solution)/shard_map/pallas_call | solution.py:394
  79.3 4.0 %shard_map.259 = (bf16[512,768]{1,0:T(8,128)(2,1)S(1)}, bf16[512,768]{1,0:T(8,128)(2,1)S(1)}, bf16[256,768]{1,0:T(8,128)(2,1)S(1)}, bf16[256,768]{1,0:T(8,128)(2,1)}) custom-call(s32[2]{0:T(128)S(1)} %pad_add_fusion.meta.refs_0_, bf16[512,768]{1,0:T(8,128)(2,1)S(1)} %get-tuple-element.72.second, bf16[512,192]{1,0:T(8,128)(2,1)S(1)} %get-tuple-element.73.att.refs_5_, ...), custom_call_target="tpu_custom_call" | custom-call | flops 3000000000 | bytes 6884352 | tf_op jit(solution)/shard_map/pallas_call | solution.py:394
  84.0 4.3 %collective-permute-done.25.cot_b.refs_2_ = bf16[256,768]{1,0:T(8,128)(2,1)S(1)} collective-permute-done((bf16[256,768]{1,0:T(8,128)(2,1)S(1)}, bf16[256,768]{1,0:T(8,128)(2,1)S(1)}, u32[]{:S(2)}, u32[]{:S(2)}) %collective-permute-start.25) | collective-permute-done | bytes 393248 | tf_op jit(solution)/shard_map/ppermute | solution.py:49
  88.4 3.4 %shard_map.261 = (bf16[512,768]{1,0:T(8,128)(2,1)S(1)}, f32[768,768]{1,0:T(8,128)S(1)}, f32[768,768]{1,0:T(8,128)S(1)}, f32[8,768]{1,0:T(8,128)S(1)}, f32[8,768]{1,0:T(8,128)S(1)}) custom-call(s32[2]{0:T(128)S(1)} %pad_add_fusion.meta.refs_0_, bf16[256,768]{1,0:T(8,128)(2,1)S(1)} %collective-permute-done.24.cot_a.refs_1_, ...), custom_call_target="tpu_custom_call" | custom-call | flops 5000000000 | bytes 11864064 | tf_op jit(solution)/shard_map/pallas_call | solution.py:394
  91.8 8.8 %shard_map.263 = (bf16[256,768]{1,0:T(8,128)(2,1)S(1)}, bf16[256,768]{1,0:T(8,128)(2,1)}, f32[8,768]{1,0:T(8,128)S(1)}, f32[8,640]{1,0:T(8,128)S(1)}, f32[768,576]{1,0:T(8,128)S(1)}, /*index=5*/f32[768,192]{1,0:T(8,128)S(1)}) custom-call(s32[2]{0:T(128)S(1)} %pad_add_fusion.meta.refs_0_, bf16[256,768]{1,0:T(8,128)(2,1)S(1)} %collective-permute-done.24.cot_a.refs_1_, ...), custom_call_target="tpu_custom_call" | custom-call | flops 8999999488 | bytes 10352640 | tf_op jit(solution)/shard_map/pallas_call | solution.py:394
  101.3 3.8 %shard_map.262 = (bf16[512,768]{1,0:T(8,128)(2,1)S(1)}, f32[4,96,1536]{2,1,0:T(8,128)S(1)}, bf16[4,96,1536]{2,1,0:T(8,128)(2,1)S(1)}, f32[8,768]{1,0:T(8,128)S(1)}, f32[8,768]{1,0:T(8,128)S(1)}) custom-call(s32[2]{0:T(128)S(1)} %pad_add_fusion.meta.refs_0_, bf16[256,768]{1,0:T(8,128)(2,1)S(1)} %get-tuple-element.76.cot_a.refs_1_, ...), custom_call_target="tpu_custom_call" | custom-call | flops 5000000000 | bytes 15452160 | tf_op jit(solution)/shard_map/pallas_call | solution.py:394
  105.1 8.5 %shard_map.264 = (bf16[256,768]{1,0:T(8,128)(2,1)S(1)}, bf16[256,768]{1,0:T(8,128)(2,1)S(1)}, f32[8,768]{1,0:T(8,128)S(1)}, f32[8,640]{1,0:T(8,128)S(1)}, f32[76...) custom-call(s32[2]{0:T(128)S(1)} %pad_add_fusion.meta.refs_0_, bf16[256,768]{1,0:T(8,128)(2,1)S(1)} %get-tuple-element.76.cot_a.refs_1_, ...), custom_call_target="tpu_custom_call" | custom-call | flops 8999999488 | bytes 12756992 | tf_op jit(solution)/shard_map/pallas_call | solution.py:394
  113.6 1.9 %shard_map.266 = (f32[4,96,896]{2,1,0:T(8,128)S(1)}, bf16[4,96,896]{2,1,0:T(8,128)(2,1)}) custom-call(s32[2]{0:T(128)S(1)} %pad_add_fusion.meta.refs_0_, f32[768,576]{1,0:T(8,128)S(1)} %get-tuple-element.103.gqkv, f32[768,192]{1,0:T(8,128)S(1)} %get-tuple-element.104.gdense, f32[8,768]{1,0:T(8,128)S(1)} %get-tuple-element.105.stat, ...), custom_call_target="tpu_custom_call" | custom-call | flops 1000000000 | bytes 4542464 | tf_op jit(solution)/shard_map/pallas_call | solution.py:394
  115.6 1.1 copy-done
  117.6 2.1 %collective-permute-start.18 = (bf16[256,768]{1,0:T(8,128)(2,1)}, bf16[256,768]{1,0:T(8,128)(2,1)S(1)}, u32[]{:S(2)}, u32[]{:S(2)}) collective-permute-start(bf16[256,768]{1,0:T(8,128)(2,1)} %copy-done.12), channel_id=1, source_target_pairs={{0,1},{1,0},{2,3},{3,2},{4,5},{5,4},{6,7},{7,6},{8,9},{9,8},{10,11... | collective-permute-start | bytes 1179656 | tf_op jit(solution)/shard_map/ppermute | solution.py:49
  119.7 1.2 add_convert_fusion.1
  121.0 8.0 %collective-permute-done.27 = bf16[256,768]{1,0:T(8,128)(2,1)} collective-permute-done((bf16[256,768]{1,0:T(8,128)(2,1)}, bf16[256,768]{1,0:T(8,128)(2,1)}, u32[]{:S(2)}, u32[]{:S(2)}) %collective-permute-start.27) | collective-permute-done | bytes 393248 | tf_op jit(solution)/shard_map/ppermute | solution.py:49
  130.0 1.3 add_convert_fusion
  131.2 2.0 %collective-permute-start.28 = (bf16[256,768]{1,0:T(8,128)(2,1)S(1)}, bf16[256,768]{1,0:T(8,128)(2,1)S(1)}, u32[]{:S(2)}, u32[]{:S(2)}) collective-permute-start(bf16[256,768]{1,0:T(8,128)(2,1)S(1)} %add_convert_fusion), channel_id=1, source_target_pairs={{0,2},{1,3},{2,0},{3,1},{4,6},{5,7},{6,4},{7,5},{8,10},{9,11},{10,... | collective-permute-start | bytes 1179656 | tf_op jit(solution)/shard_map/ppermute | solution.py:49
  133.3 1.2 fusion.13
  134.4 17.2 %collective-permute-done.18 = bf16[256,768]{1,0:T(8,128)(2,1)S(1)} collective-permute-done((bf16[256,768]{1,0:T(8,128)(2,1)}, bf16[256,768]{1,0:T(8,128)(2,1)S(1)}, u32[]{:S(2)}, u32[]{:S(2)}) %collective-permute-start.18) | collective-permute-done | bytes 393248 | tf_op jit(solution)/shard_map/ppermute | solution.py:49
  151.7 1.7 collective-permute-start.30
  153.3 1.3 collective-permute-start.32
  154.6 1.1 add_add_fusion
  155.7 3.9 %collective-permute-done.26.one = bf16[256,768]{1,0:T(8,128)(2,1)S(1)} collective-permute-done((bf16[256,768]{1,0:T(8,128)(2,1)}, bf16[256,768]{1,0:T(8,128)(2,1)S(1)}, u32[]{:S(2)}, u32[]{:S(2)}) %collective-permute-start.26) | collective-permute-done | bytes 393248 | tf_op jit(solution)/shard_map/ppermute | solution.py:49
  159.6 1.5 collective-permute-start.31
  161.1 4.3 %collective-permute-done.28.two = bf16[256,768]{1,0:T(8,128)(2,1)S(1)} collective-permute-done((bf16[256,768]{1,0:T(8,128)(2,1)S(1)}, bf16[256,768]{1,0:T(8,128)(2,1)S(1)}, u32[]{:S(2)}, u32[]{:S(2)}) %collective-permute-start.28) | collective-permute-done | bytes 393248 | tf_op jit(solution)/shard_map/ppermute | solution.py:49
  165.4 2.0 %shard_map.265 = f32[256,768]{1,0:T(8,128)} custom-call(s32[2]{0:T(128)S(1)} %pad_add_fusion.meta.refs_0_, bf16[256,768]{1,0:T(8,128)(2,1)S(1)} %copy-done.15, bf16[256,768]{1,0:T(8,128)(2,1)S(1)} %collective-permute-done.26.one, bf16[256,768]{1,0:T(8,128)(2,1)S(1)} %collective-permute-done.28.two, bf16[256,768]{1,0:T(8,128)(2,1)S(1)} %copy-done.3, ...), custom_call_target="tpu_custom_call" | custom-call | flops 2000000000 | bytes 3145728 | tf_op jit(solution)/shard_map/pallas_call | solution.py:394
  168.5 2.5 %collective-permute-start.35 = (f32[96,128]{1,0:T(8,128)S(1)}, f32[96,128]{1,0:T(8,128)S(1)}, u32[]{:S(2)}, u32[]{:S(2)}) collective-permute-start(f32[96,128]{1,0:T(8,128)S(1)} %slice.131), channel_id=1, source_target_pairs={{0,3},{1,2},{2,1},{3,0},{4,7},{5,6},{6,5},{7,4},{8,11},{9,10},{10,... | collective-permute-start | bytes 147464 | tf_op jit(solution)/shard_map/ppermute | solution.py:49
  171.0 2.0 %collective-permute-start.33 = (f32[96,128]{1,0:T(8,128)S(1)}, f32[96,128]{1,0:T(8,128)S(1)}, u32[]{:S(2)}, u32[]{:S(2)}) collective-permute-start(f32[96,128]{1,0:T(8,128)S(1)} %slice.131), channel_id=1, source_target_pairs={{0,1},{1,0},{2,3},{3,2},{4,5},{5,4},{6,7},{7,6},{8,9},{9,8},{10,11... | collective-permute-start | bytes 147464 | tf_op jit(solution)/shard_map/ppermute | solution.py:49
  173.2 1.2 fusion.4
  174.4 1.7 collective-permute-start.37
  176.1 1.3 collective-permute-start.39
  181.7 3.5 %collective-permute-done.37 = bf16[96,1536]{1,0:T(8,128)(2,1)S(1)} collective-permute-done((bf16[96,1536]{1,0:T(8,128)(2,1)}, bf16[96,1536]{1,0:T(8,128)(2,1)S(1)}, u32[]{:S(2)}, u32[]{:S(2)}) %collective-permute-start.37) | collective-permute-done | bytes 294944 | tf_op jit(solution)/shard_map/ppermute | solution.py:49
  185.2 3.1 %collective-permute-done.39 = bf16[96,1536]{1,0:T(8,128)(2,1)S(1)} collective-permute-done((bf16[96,1536]{1,0:T(8,128)(2,1)}, bf16[96,1536]{1,0:T(8,128)(2,1)S(1)}, u32[]{:S(2)}, u32[]{:S(2)}) %collective-permute-start.39) | collective-permute-done | bytes 294944 | tf_op jit(solution)/shard_map/ppermute | solution.py:49
  188.4 1.2 fusion.1
  (121 shorter events, 24.7 us)
Async XLA Ops:
  0.6 28.1 %copy-start.2 = (f32[256,768]{1,0:T(8,128)S(1)}, f32[256,768]{1,0:T(8,128)}, u32[]{:S(2)}) copy-start(f32[256,768]{1,0:T(8,128)} %cot.3) | copy-start | bytes 2359300
  1.5 9.3 %collective-permute-start.3 = (f32[6,24]{1,0:T(8,128)S(1)}, f32[6,24]{1,0:T(8,128)S(1)}, u32[]{:S(2)}, u32[]{:S(2)}) collective-permute-start(f32[6,24]{1,0:T(8,128)S(1)} %stack.45), channel_id=1, source_target_pairs={{0,1},{1,0},{2,3},{3,2},{4,5},{5,4},{6,7},{7,6},{8,9},{9,8},{10,11... | collective-permute-start | bytes 1736 | tf_op jit(solution)/shard_map/ppermute | solution.py:49
  4.6 6.2 %collective-permute-start.2 = (f32[6,24]{1,0:T(8,128)S(1)}, f32[6,24]{1,0:T(8,128)S(1)}, u32[]{:S(2)}, u32[]{:S(2)}) collective-permute-start(f32[6,24]{1,0:T(8,128)S(1)} %stack.45), channel_id=1, source_target_pairs={{0,2},{1,3},{2,0},{3,1},{4,6},{5,7},{6,4},{7,5},{8,10},{9,11},{10,... | collective-permute-start | bytes 1736 | tf_op jit(solution)/shard_map/ppermute | solution.py:49
  7.2 5.4 %collective-permute-start.1 = (f32[6,24]{1,0:T(8,128)S(1)}, f32[6,24]{1,0:T(8,128)S(1)}, u32[]{:S(2)}, u32[]{:S(2)}) collective-permute-start(f32[6,24]{1,0:T(8,128)S(1)} %stack.45), channel_id=1, source_target_pairs={{0,3},{1,2},{2,1},{3,0},{4,7},{5,6},{6,5},{7,4},{8,11},{9,10},{10,... | collective-permute-start | bytes 1736 | tf_op jit(solution)/shard_map/ppermute | solution.py:49
  8.2 16.6 %collective-permute-start.14 = (bf16[96,1536]{1,0:T(8,128)(2,1)S(1)}, bf16[96,1536]{1,0:T(8,128)(2,1)S(1)}, u32[]{:S(2)}, u32[]{:S(2)}) collective-permute-start(bf16[96,1536]{1,0:T(8,128)(2,1)S(1)} %pad_maximum_fusion.1.refs_0_), channel_id=1, source_target_pairs={{0,4},{4,0},{8,12},{12,8},{16,20},{20,16},{24,28},{28,24},{1,5},{5... | collective-permute-start | bytes 884744 | tf_op jit(solution)/shard_map/ppermute | solution.py:49
  13.8 7.9 %collective-permute-start.6 = (bf16[112,768]{1,0:T(8,128)(2,1)S(1)}, bf16[112,768]{1,0:T(8,128)(2,1)S(1)}, u32[]{:S(2)}, u32[]{:S(2)}) collective-permute-start(bf16[112,768]{1,0:T(8,128)(2,1)S(1)} %pad_maximum_fusion.2.refs_0_), channel_id=1, source_target_pairs={{0,24},{4,28},{8,16},{12,20},{16,8},{20,12},{24,0},{28,4},{1,25},{... | collective-permute-start | bytes 516104 | tf_op jit(solution)/shard_map/ppermute | solution.py:49
  16.3 7.1 %collective-permute-start.5 = (bf16[112,768]{1,0:T(8,128)(2,1)S(1)}, bf16[112,768]{1,0:T(8,128)(2,1)S(1)}, u32[]{:S(2)}, u32[]{:S(2)}) collective-permute-start(bf16[112,768]{1,0:T(8,128)(2,1)S(1)} %pad_maximum_fusion.2.refs_0_), channel_id=1, source_target_pairs={{0,16},{4,20},{8,24},{12,28},{16,0},{20,4},{24,8},{28,12},{1,17},{... | collective-permute-start | bytes 516104 | tf_op jit(solution)/shard_map/ppermute | solution.py:49
  16.8 6.9 %collective-permute-start.4 = (bf16[112,768]{1,0:T(8,128)(2,1)S(1)}, bf16[112,768]{1,0:T(8,128)(2,1)S(1)}, u32[]{:S(2)}, u32[]{:S(2)}) collective-permute-start(bf16[112,768]{1,0:T(8,128)(2,1)S(1)} %pad_maximum_fusion.2.refs_0_), channel_id=1, source_target_pairs={{0,8},{4,12},{8,0},{12,4},{16,24},{20,28},{24,16},{28,20},{1,9},{5... | collective-permute-start | bytes 516104 | tf_op jit(solution)/shard_map/ppermute | solution.py:49
  17.3 6.6 %collective-permute-start.7 = (bf16[112,768]{1,0:T(8,128)(2,1)S(1)}, bf16[112,768]{1,0:T(8,128)(2,1)S(1)}, u32[]{:S(2)}, u32[]{:S(2)}) collective-permute-start(bf16[112,768]{1,0:T(8,128)(2,1)S(1)} %pad_maximum_fusion.2.refs_0_), channel_id=1, source_target_pairs={{0,4},{4,0},{8,12},{12,8},{16,20},{20,16},{24,28},{28,24},{1,5},{5... | collective-permute-start | bytes 516104 | tf_op jit(solution)/shard_map/ppermute | solution.py:49
  21.6 7.7 %collective-permute-start.10 = (bf16[112,768]{1,0:T(8,128)(2,1)S(1)}, bf16[112,768]{1,0:T(8,128)(2,1)S(1)}, u32[]{:S(2)}, u32[]{:S(2)}) collective-permute-start(bf16[112,768]{1,0:T(8,128)(2,1)S(1)} %collective-permute-done.6.refs_3_), channel_id=1, source_target_pairs={{0,4},{4,0},{8,12},{12,8},{16,20},{20,16},{24,28},{28,24},{1,5},{5... | collective-permute-start | bytes 516104 | tf_op jit(solution)/shard_map/ppermute | solution.py:49
  23.4 7.8 %collective-permute-start.9 = (bf16[112,768]{1,0:T(8,128)(2,1)S(1)}, bf16[112,768]{1,0:T(8,128)(2,1)S(1)}, u32[]{:S(2)}, u32[]{:S(2)}) collective-permute-start(bf16[112,768]{1,0:T(8,128)(2,1)S(1)} %collective-permute-done.5.refs_2_), channel_id=1, source_target_pairs={{0,4},{4,0},{8,12},{12,8},{16,20},{20,16},{24,28},{28,24},{1,5},{5... | collective-permute-start | bytes 516104 | tf_op jit(solution)/shard_map/ppermute | solution.py:49
  23.6 8.8 %collective-permute-start.8 = (bf16[112,768]{1,0:T(8,128)(2,1)S(1)}, bf16[112,768]{1,0:T(8,128)(2,1)S(1)}, u32[]{:S(2)}, u32[]{:S(2)}) collective-permute-start(bf16[112,768]{1,0:T(8,128)(2,1)S(1)} %collective-permute-done.4.refs_1_), channel_id=1, source_target_pairs={{0,4},{4,0},{8,12},{12,8},{16,20},{20,16},{24,28},{28,24},{1,5},{5... | collective-permute-start | bytes 516104 | tf_op jit(solution)/shard_map/ppermute | solution.py:49
  23.9 21.7 %collective-permute-start = (bf16[256,768]{1,0:T(8,128)(2,1)}, bf16[256,768]{1,0:T(8,128)(2,1)}, u32[]{:S(2)}, u32[]{:S(2)}) collective-permute-start(bf16[256,768]{1,0:T(8,128)(2,1)} %hid.1), channel_id=1, source_target_pairs={{0,1},{1,0},{2,3},{3,2},{4,5},{5,4},{6,7},{7,6},{8,9},{9,8},{10,11... | collective-permute-start | bytes 1179656 | tf_op jit(solution)/shard_map/ppermute | solution.py:49
  24.8 30.1 %collective-permute-start.19 = (bf16[256,768]{1,0:T(8,128)(2,1)}, bf16[256,768]{1,0:T(8,128)(2,1)}, u32[]{:S(2)}, u32[]{:S(2)}) collective-permute-start(bf16[256,768]{1,0:T(8,128)(2,1)} %hid.1), channel_id=1, source_target_pairs={{0,2},{1,3},{2,0},{3,1},{4,6},{5,7},{6,4},{7,5},{8,10},{9,11},{10,... | collective-permute-start | bytes 1179656 | tf_op jit(solution)/shard_map/ppermute | solution.py:49
  29.4 10.9 %collective-permute-start.13 = (bf16[96,1536]{1,0:T(8,128)(2,1)S(1)}, bf16[96,1536]{1,0:T(8,128)(2,1)S(1)}, u32[]{:S(2)}, u32[]{:S(2)}) collective-permute-start(bf16[96,1536]{1,0:T(8,128)(2,1)S(1)} %pad_maximum_fusion.1.refs_0_), channel_id=1, source_target_pairs={{0,24},{4,28},{8,16},{12,20},{16,8},{20,12},{24,0},{28,4},{1,25},{... | collective-permute-start | bytes 884744 | tf_op jit(solution)/shard_map/ppermute | solution.py:49
  31.2 13.9 %collective-permute-start.12 = (bf16[96,1536]{1,0:T(8,128)(2,1)S(1)}, bf16[96,1536]{1,0:T(8,128)(2,1)S(1)}, u32[]{:S(2)}, u32[]{:S(2)}) collective-permute-start(bf16[96,1536]{1,0:T(8,128)(2,1)S(1)} %pad_maximum_fusion.1.refs_0_), channel_id=1, source_target_pairs={{0,16},{4,20},{8,24},{12,28},{16,0},{20,4},{24,8},{28,12},{1,17},{... | collective-permute-start | bytes 884744 | tf_op jit(solution)/shard_map/ppermute | solution.py:49
  32.4 12.8 %collective-permute-start.11 = (bf16[96,1536]{1,0:T(8,128)(2,1)S(1)}, bf16[96,1536]{1,0:T(8,128)(2,1)S(1)}, u32[]{:S(2)}, u32[]{:S(2)}) collective-permute-start(bf16[96,1536]{1,0:T(8,128)(2,1)S(1)} %pad_maximum_fusion.1.refs_0_), channel_id=1, source_target_pairs={{0,8},{4,12},{8,0},{12,4},{16,24},{20,28},{24,16},{28,20},{1,9},{5... | collective-permute-start | bytes 884744 | tf_op jit(solution)/shard_map/ppermute | solution.py:49
  34.0 21.1 %copy-start.3 = (bf16[256,768]{1,0:T(8,128)(2,1)S(1)}, bf16[256,768]{1,0:T(8,128)(2,1)}, u32[]{:S(2)}) copy-start(bf16[256,768]{1,0:T(8,128)(2,1)} %hid.1) | copy-start | bytes 1179652
  37.5 67.6 %copy-start.10 = (f32[6,768]{1,0:T(8,128)}, f32[6,768]{1,0:T(8,128)S(1)}, u32[]{:S(2)}) copy-start(f32[6,768]{1,0:T(8,128)S(1)} %get-tuple-element.64.gains.refs_9_) | copy-start | bytes 55300
  40.3 22.8 %collective-permute-start.24 = (bf16[256,768]{1,0:T(8,128)(2,1)S(1)}, bf16[256,768]{1,0:T(8,128)(2,1)S(1)}, u32[]{:S(2)}, u32[]{:S(2)}) collective-permute-start(bf16[256,768]{1,0:T(8,128)(2,1)S(1)} %get-tuple-element.76.cot_a.refs_1_), channel_id=1, source_target_pairs={{0,2},{1,3},{2,0},{3,1},{4,6},{5,7},{6,4},{7,5},{8,10},{9,11},{10,... | collective-permute-start | bytes 1179656 | tf_op jit(solution)/shard_map/ppermute | solution.py:49
  45.1 19.7 %collective-permute-start.17 = (bf16[96,1536]{1,0:T(8,128)(2,1)S(1)}, bf16[96,1536]{1,0:T(8,128)(2,1)S(1)}, u32[]{:S(2)}, u32[]{:S(2)}) collective-permute-start(bf16[96,1536]{1,0:T(8,128)(2,1)S(1)} %collective-permute-done.13.refs_3_), channel_id=1, source_target_pairs={{0,4},{4,0},{8,12},{12,8},{16,20},{20,16},{24,28},{28,24},{1,5},{5... | collective-permute-start | bytes 884744 | tf_op jit(solution)/shard_map/ppermute | solution.py:49
  45.2 19.9 %collective-permute-start.16 = (bf16[96,1536]{1,0:T(8,128)(2,1)S(1)}, bf16[96,1536]{1,0:T(8,128)(2,1)S(1)}, u32[]{:S(2)}, u32[]{:S(2)}) collective-permute-start(bf16[96,1536]{1,0:T(8,128)(2,1)S(1)} %collective-permute-done.12.refs_2_), channel_id=1, source_target_pairs={{0,4},{4,0},{8,12},{12,8},{16,20},{20,16},{24,28},{28,24},{1,5},{5... | collective-permute-start | bytes 884744 | tf_op jit(solution)/shard_map/ppermute | solution.py:49
  45.6 19.5 %collective-permute-start.15 = (bf16[96,1536]{1,0:T(8,128)(2,1)S(1)}, bf16[96,1536]{1,0:T(8,128)(2,1)S(1)}, u32[]{:S(2)}, u32[]{:S(2)}) collective-permute-start(bf16[96,1536]{1,0:T(8,128)(2,1)S(1)} %collective-permute-done.11.refs_1_), channel_id=1, source_target_pairs={{0,4},{4,0},{8,12},{12,8},{16,20},{20,16},{24,28},{28,24},{1,5},{5... | collective-permute-start | bytes 884744 | tf_op jit(solution)/shard_map/ppermute | solution.py:49
  54.9 16.6 %collective-permute-start.20 = (bf16[256,768]{1,0:T(8,128)(2,1)}, bf16[256,768]{1,0:T(8,128)(2,1)S(1)}, u32[]{:S(2)}, u32[]{:S(2)}) collective-permute-start(bf16[256,768]{1,0:T(8,128)(2,1)} %collective-permute-done.19.hid_a), channel_id=1, source_target_pairs={{0,1},{1,0},{2,3},{3,2},{4,5},{5,4},{6,7},{7,6},{8,9},{9,8},{10,11... | collective-permute-start | bytes 1179656 | tf_op jit(solution)/shard_map/ppermute | solution.py:49
  63.1 38.2 %collective-permute-start.23 = (bf16[256,768]{1,0:T(8,128)(2,1)S(1)}, bf16[256,768]{1,0:T(8,128)(2,1)S(1)}, u32[]{:S(2)}, u32[]{:S(2)}) collective-permute-start(bf16[256,768]{1,0:T(8,128)(2,1)S(1)} %get-tuple-element.76.cot_a.refs_1_), channel_id=1, source_target_pairs={{0,1},{1,0},{2,3},{3,2},{4,5},{5,4},{6,7},{7,6},{8,9},{9,8},{10,11... | collective-permute-start | bytes 1179656 | tf_op jit(solution)/shard_map/ppermute | solution.py:49
  64.8 23.5 %collective-permute-start.25 = (bf16[256,768]{1,0:T(8,128)(2,1)S(1)}, bf16[256,768]{1,0:T(8,128)(2,1)S(1)}, u32[]{:S(2)}, u32[]{:S(2)}) collective-permute-start(bf16[256,768]{1,0:T(8,128)(2,1)S(1)} %collective-permute-done.24.cot_a.refs_1_), channel_id=1, source_target_pairs={{0,1},{1,0},{2,3},{3,2},{4,5},{5,4},{6,7},{7,6},{8,9},{9,8},{10,11... | collective-permute-start | bytes 1179656 | tf_op jit(solution)/shard_map/ppermute | solution.py:49
  69.6 9.7 %copy-start.12 = (bf16[256,768]{1,0:T(8,128)(2,1)}, bf16[256,768]{1,0:T(8,128)(2,1)S(1)}, u32[]{:S(2)}) copy-start(bf16[256,768]{1,0:T(8,128)(2,1)S(1)} %get-tuple-element.71) | copy-start | bytes 1179652
  84.0 35.7 %collective-permute-start.21 = (bf16[256,768]{1,0:T(8,128)(2,1)}, bf16[256,768]{1,0:T(8,128)(2,1)}, u32[]{:S(2)}, u32[]{:S(2)}) collective-permute-start(bf16[256,768]{1,0:T(8,128)(2,1)} %get-tuple-element.75), channel_id=1, source_target_pairs={{0,1},{1,0},{2,3},{3,2},{4,5},{5,4},{6,7},{7,6},{8,9},{9,8},{10,11... | collective-permute-start | bytes 1179656 | tf_op jit(solution)/shard_map/ppermute | solution.py:49
  116.7 14.5 %collective-permute-start.29 = (bf16[4,96,896]{2,1,0:T(8,128)(2,1)}, bf16[4,96,896]{2,1,0:T(8,128)(2,1)}, u32[]{:S(2)}, u32[]{:S(2)}) collective-permute-start(bf16[4,96,896]{2,1,0:T(8,128)(2,1)} %get-tuple-element.111), channel_id=1, source_target_pairs={{0,4},{4,0},{8,12},{12,8},{16,20},{20,16},{24,28},{28,24},{1,5},{5... | collective-permute-start | bytes 2064392 | tf_op jit(solution)/shard_map/ppermute | solution.py:49
  116.7 12.3 %collective-permute-start.27 = (bf16[256,768]{1,0:T(8,128)(2,1)}, bf16[256,768]{1,0:T(8,128)(2,1)}, u32[]{:S(2)}, u32[]{:S(2)}) collective-permute-start(bf16[256,768]{1,0:T(8,128)(2,1)} %get-tuple-element.102), channel_id=1, source_target_pairs={{0,1},{1,0},{2,3},{3,2},{4,5},{5,4},{6,7},{7,6},{8,9},{9,8},{10,11... | collective-permute-start | bytes 1179656 | tf_op jit(solution)/shard_map/ppermute | solution.py:49
  116.7 16.6 %copy-start.1 = (f32[4,96,896]{2,1,0:T(8,128)S(1)}, f32[4,96,896]{2,1,0:T(8,128)}, u32[]{:S(2)}) copy-start(f32[4,96,896]{2,1,0:T(8,128)} %copy-done) | copy-start | bytes 4128772
  117.6 34.1 %collective-permute-start.18 = (bf16[256,768]{1,0:T(8,128)(2,1)}, bf16[256,768]{1,0:T(8,128)(2,1)S(1)}, u32[]{:S(2)}, u32[]{:S(2)}) collective-permute-start(bf16[256,768]{1,0:T(8,128)(2,1)} %copy-done.12), channel_id=1, source_target_pairs={{0,1},{1,0},{2,3},{3,2},{4,5},{5,4},{6,7},{7,6},{8,9},{9,8},{10,11... | collective-permute-start | bytes 1179656 | tf_op jit(solution)/shard_map/ppermute | solution.py:49
  119.7 40.0 %collective-permute-start.26 = (bf16[256,768]{1,0:T(8,128)(2,1)}, bf16[256,768]{1,0:T(8,128)(2,1)S(1)}, u32[]{:S(2)}, u32[]{:S(2)}) collective-permute-start(bf16[256,768]{1,0:T(8,128)(2,1)} %copy-done.13), channel_id=1, source_target_pairs={{0,1},{1,0},{2,3},{3,2},{4,5},{5,4},{6,7},{7,6},{8,9},{9,8},{10,11... | collective-permute-start | bytes 1179656 | tf_op jit(solution)/shard_map/ppermute | solution.py:49
  119.7 53.5 %collective-permute-start.36 = (bf16[4,96,1536]{2,1,0:T(8,128)(2,1)}, bf16[4,96,1536]{2,1,0:T(8,128)(2,1)S(1)}, u32[]{:S(2)}, u32[]{:S(2)}) collective-permute-start(bf16[4,96,1536]{2,1,0:T(8,128)(2,1)} %copy-done.11), channel_id=1, source_target_pairs={{0,4},{4,0},{8,12},{12,8},{16,20},{20,16},{24,28},{28,24},{1,5},{5... | collective-permute-start | bytes 3538952 | tf_op jit(solution)/shard_map/ppermute | solution.py:49
  129.0 24.3 %collective-permute-start.22 = (bf16[256,768]{1,0:T(8,128)(2,1)S(1)}, bf16[256,768]{1,0:T(8,128)(2,1)S(1)}, u32[]{:S(2)}, u32[]{:S(2)}) collective-permute-start(bf16[256,768]{1,0:T(8,128)(2,1)S(1)} %add_convert_fusion.1), channel_id=1, source_target_pairs={{0,2},{1,3},{2,0},{3,1},{4,6},{5,7},{6,4},{7,5},{8,10},{9,11},{10,... | collective-permute-start | bytes 1179656 | tf_op jit(solution)/shard_map/ppermute | solution.py:49
  130.0 24.7 %copy-start.5 = (bf16[256,768]{1,0:T(8,128)(2,1)S(1)}, bf16[256,768]{1,0:T(8,128)(2,1)}, u32[]{:S(2)}) copy-start(bf16[256,768]{1,0:T(8,128)(2,1)} %copy-done.4) | copy-start | bytes 1179652
  131.2 34.2 %collective-permute-start.28 = (bf16[256,768]{1,0:T(8,128)(2,1)S(1)}, bf16[256,768]{1,0:T(8,128)(2,1)S(1)}, u32[]{:S(2)}, u32[]{:S(2)}) collective-permute-start(bf16[256,768]{1,0:T(8,128)(2,1)S(1)} %add_convert_fusion), channel_id=1, source_target_pairs={{0,2},{1,3},{2,0},{3,1},{4,6},{5,7},{6,4},{7,5},{8,10},{9,11},{10,... | collective-permute-start | bytes 1179656 | tf_op jit(solution)/shard_map/ppermute | solution.py:49
  134.4 31.0 %copy-start.15 = (bf16[256,768]{1,0:T(8,128)(2,1)S(1)}, bf16[256,768]{1,0:T(8,128)(2,1)}, u32[]{:S(2)}) copy-start(bf16[256,768]{1,0:T(8,128)(2,1)} %copy-done.14) | copy-start | bytes 1179652
  151.7 15.8 %collective-permute-start.30 = (bf16[96,896]{1,0:T(8,128)(2,1)S(1)}, bf16[96,896]{1,0:T(8,128)(2,1)S(1)}, u32[]{:S(2)}, u32[]{:S(2)}) collective-permute-start(bf16[96,896]{1,0:T(8,128)(2,1)S(1)} %get-tuple-element.152), channel_id=1, source_target_pairs={{0,24},{4,28},{8,16},{12,20},{16,8},{20,12},{24,0},{28,4},{1,25},{... | collective-permute-start | bytes 516104 | tf_op jit(solution)/shard_map/ppermute | solution.py:49
  153.3 14.1 %collective-permute-start.32 = (bf16[96,896]{1,0:T(8,128)(2,1)S(1)}, bf16[96,896]{1,0:T(8,128)(2,1)S(1)}, u32[]{:S(2)}, u32[]{:S(2)}) collective-permute-start(bf16[96,896]{1,0:T(8,128)(2,1)S(1)} %get-tuple-element.153), channel_id=1, source_target_pairs={{0,16},{4,20},{8,24},{12,28},{16,0},{20,4},{24,8},{28,12},{1,17},{... | collective-permute-start | bytes 516104 | tf_op jit(solution)/shard_map/ppermute | solution.py:49
  159.6 7.8 %collective-permute-start.31 = (bf16[96,896]{1,0:T(8,128)(2,1)S(1)}, bf16[96,896]{1,0:T(8,128)(2,1)S(1)}, u32[]{:S(2)}, u32[]{:S(2)}) collective-permute-start(bf16[96,896]{1,0:T(8,128)(2,1)S(1)} %get-tuple-element.154), channel_id=1, source_target_pairs={{0,8},{4,12},{8,0},{12,4},{16,24},{20,28},{24,16},{28,20},{1,9},{5... | collective-permute-start | bytes 516104 | tf_op jit(solution)/shard_map/ppermute | solution.py:49
  168.5 8.9 %collective-permute-start.35 = (f32[96,128]{1,0:T(8,128)S(1)}, f32[96,128]{1,0:T(8,128)S(1)}, u32[]{:S(2)}, u32[]{:S(2)}) collective-permute-start(f32[96,128]{1,0:T(8,128)S(1)} %slice.131), channel_id=1, source_target_pairs={{0,3},{1,2},{2,1},{3,0},{4,7},{5,6},{6,5},{7,4},{8,11},{9,10},{10,... | collective-permute-start | bytes 147464 | tf_op jit(solution)/shard_map/ppermute | solution.py:49
  171.0 9.9 %collective-permute-start.34 = (f32[96,128]{1,0:T(8,128)S(1)}, f32[96,128]{1,0:T(8,128)S(1)}, u32[]{:S(2)}, u32[]{:S(2)}) collective-permute-start(f32[96,128]{1,0:T(8,128)S(1)} %slice.131), channel_id=1, source_target_pairs={{0,2},{1,3},{2,0},{3,1},{4,6},{5,7},{6,4},{7,5},{8,10},{9,11},{10,... | collective-permute-start | bytes 147464 | tf_op jit(solution)/shard_map/ppermute | solution.py:49
  171.0 9.9 %collective-permute-start.33 = (f32[96,128]{1,0:T(8,128)S(1)}, f32[96,128]{1,0:T(8,128)S(1)}, u32[]{:S(2)}, u32[]{:S(2)}) collective-permute-start(f32[96,128]{1,0:T(8,128)S(1)} %slice.131), channel_id=1, source_target_pairs={{0,1},{1,0},{2,3},{3,2},{4,5},{5,4},{6,7},{7,6},{8,9},{9,8},{10,11... | collective-permute-start | bytes 147464 | tf_op jit(solution)/shard_map/ppermute | solution.py:49
  174.4 10.8 %collective-permute-start.37 = (bf16[96,1536]{1,0:T(8,128)(2,1)}, bf16[96,1536]{1,0:T(8,128)(2,1)S(1)}, u32[]{:S(2)}, u32[]{:S(2)}) collective-permute-start(bf16[96,1536]{1,0:T(8,128)(2,1)} %get-tuple-element.149), channel_id=1, source_target_pairs={{0,24},{4,28},{8,16},{12,20},{16,8},{20,12},{24,0},{28,4},{1,25},{... | collective-permute-start | bytes 884744 | tf_op jit(solution)/shard_map/ppermute | solution.py:49
  176.1 12.2 %collective-permute-start.39 = (bf16[96,1536]{1,0:T(8,128)(2,1)}, bf16[96,1536]{1,0:T(8,128)(2,1)S(1)}, u32[]{:S(2)}, u32[]{:S(2)}) collective-permute-start(bf16[96,1536]{1,0:T(8,128)(2,1)} %get-tuple-element.150), channel_id=1, source_target_pairs={{0,16},{4,20},{8,24},{12,28},{16,0},{20,4},{24,8},{28,12},{1,17},{... | collective-permute-start | bytes 884744 | tf_op jit(solution)/shard_map/ppermute | solution.py:49
  177.4 11.1 %collective-permute-start.38 = (bf16[96,1536]{1,0:T(8,128)(2,1)S(1)}, bf16[96,1536]{1,0:T(8,128)(2,1)}, u32[]{:S(2)}, u32[]{:S(2)}) collective-permute-start(bf16[96,1536]{1,0:T(8,128)(2,1)S(1)} %get-tuple-element.151), channel_id=1, source_target_pairs={{0,8},{4,12},{8,0},{12,4},{16,24},{20,28},{24,16},{28,20},{1,9},{5... | collective-permute-start | bytes 884744 | tf_op jit(solution)/shard_map/ppermute | solution.py:49
  181.7 8.8 %copy-start.17 = (f32[24]{0:T(128)}, f32[24]{0:T(128)S(1)}, u32[]{:S(2)}) copy-start(f32[24]{0:T(128)S(1)} %get-tuple-element.202) | copy-start | bytes 292
  (10 other events, 19.4 us)
where the time goes:
time: 194 us; the launch traced here: 191 us
  waiting for transfers between devices  71.6 us (37%)
  Pallas kernels  54.8 us (28%)
  starting transfers between devices  38 us (20%)
  local copies, waits for them, and re-layouts  13.3 us (7%)
  other arithmetic  12.2 us (6%)
    ppermute x40, waiting for transfers between devices, swap(): return lax.ppermute(array, axis, [(i, i ^ bits) for i in range(size)])  71.6 us
    pallas_call x11, Pallas kernels, call(): pl.pallas_call(body, grid_spec=pltpu.PrefetchScalarGridSpec(num_scalar_pr...  51.5 us
    ppermute x40, starting transfers between devices, swap(): return lax.ppermute(array, axis, [(i, i ^ bits) for i in range(size)])  38 us
    unnamed x39, local copies, waits for them, and re-layouts  6.39 us
  transfers between devices with their start and end apart: 40, of which 17 were waited for; matrix products, arithmetic and copies ran while one was open for 9% of the time, Pallas kernels for 29%

commit v1 on v0

--- a/solution.py
+++ b/solution.py
@@ -133,6 +133,24 @@
         out_shape=outs,
         compiler_params=vmem(4),
     )(place, *blocks)
+
+
+def finish_body(meta, own, got_a, got_b, got_c, qkv_o, dense_o, qb_o, ub_o, stat_o, square, flat):
+    qcols, acols = qkv_o.shape[1], dense_o.shape[0]
+    rows = own.shape[0]
+    total = own[...] + got_a[...].astype(F32) + got_b[...].astype(F32) + got_c[...].astype(F32)
+    qkv_o[...] = total[:, :qcols]
+    flat[...] = total[:, qcols:]
+    square[...] = jnp.zeros_like(square)
+    square[:rows, :] = flat[...]
+    turned = square[...].T
+    dense_o[...] = turned[:acols, :rows]
+    stats = turned[acols : acols + 8, :]
+    stat_o[...] = stats
+    for out, row in ((qb_o, 7), (ub_o, 5)):
+        groups, per = out.shape
+        for g in range(groups):
+            out[g : g + 1, :] = stats[row : row + 1, g * per : (g + 1) * per]
 
 
 def prep_body(meta, cot, half_o, sum_o):
@@ -367,14 +385,12 @@
 
 def reduce_weights(keep, send, dp):
     if send is None:
-        total = lax.psum_scatter(keep, "dp", scatter_dimension=0, tiled=True)
-        return total[0]
+        total = lax.psum_scatter(keep, "dp", scatter_dimension=0, tiled=True)[0]
+        return [total] + [jnp.zeros_like(total)] * 3
     got = swap(send, "dp", dp, 1)
     near = [keep[j].astype(F32) + got[j].astype(F32) for j in range(keep.shape[0])]
-    total = near[0]
-    for j in (3, 1, 2):
-        total = total + swap(near[j].astype(BF), "dp", dp, 2 * j).astype(F32)
-    return total
+    parts = [swap(near[j].astype(BF), "dp", dp, 2 * j) for j in (3, 1, 2)]
+    return [near[0]] + parts
 
 
 def rotary_tables(length):
@@ -460,7 +476,9 @@
     low = small - high - middle
     triple = jnp.concatenate([high, middle, low], axis=1).astype(BF)
 
-    half_cot, cot_sum = call(prep_body, [sds((tokens, width), BF), sds((8, width))], [], meta, cotangent, mib=4)
+    half_cot, cot_sum = call(
+        prep_body, [sds((tokens, width), BF), sds((8, width))], [], meta, cotangent, mib=4
+    )
     hid_two = zswap(hidden_in, 2)
     hid_one = zswap(hidden_in, 1)
     hid_three = zswap(hid_two, 1)
@@ -475,7 +493,9 @@
     )
     pack_b = jnp.concatenate([up_weight, down_weight.T], axis=1)
     if split:
-        wa, gains, qb, ub = gather_weights(pack_a, rows, place, dp, (nvec, qcols, heads, fcols, units))
+        wa, gains, qb, ub = gather_weights(
+            pack_a, rows, place, dp, (nvec, qcols, heads, fcols, units)
+        )
         (wb,) = gather_weights(pack_b, rows, place, dp)
     else:
         every = lax.all_gather(pack_a, "dp", axis=0)
@@ -587,20 +607,26 @@
         meta, gqkv, gdense, stat_one, stat_two, cot_sum, ub_sum, qb_sum, flops=1e9,
     )
 
-    b_grad = reduce_weights(b_keep, b_send if split else None, dp)
+    b_grad = sum(a.astype(F32) for a in reduce_weights(b_keep, b_send if split else None, dp))
     grad_parts = scatter(n_near, n_far)
-    a_grad = reduce_weights(a_keep, a_send if split else None, dp)
+    lanes_up = -(-rows // 128) * 128
+    qkv_grad, dense_grad, qb_grad, ub_grad, stats = call(
+        finish_body,
+        [
+            sds((rows, qcols)), sds((acols, rows)), sds((heads, 3 * HD // dp)),
+            sds((units, fcols // units // dp)), sds((8, lanes_up)),
+        ],
+        [((lanes_up, acols + stat_lanes), F32), ((rows, acols + stat_lanes), F32)],
+        meta, *reduce_weights(a_keep, a_send if split else None, dp), mib=8, flops=1e9,
+    )
     (hidden_grad,) = call(
         final_body, [sds((tokens, width))], [], meta, *grad_parts, hidden_in, cotangent, mib=8, flops=2e9
     )
 
-    stats = a_grad[:, qcols + acols :]
-    qb_grad = stats[: heads * (3 * HD // dp), 7].reshape(heads, -1)
-    ub_grad = stats[: fcols // dp, 5].reshape(up_bias.shape[0], -1)
     total = stats
     for k in range(1, tensor):
         total = total + zswap(stats, k)
-    mine = lax.dynamic_slice_in_dim(total, z_at * part, part, 0)[:, :8].T
+    mine = lax.dynamic_slice_in_dim(total, z_at * part, part, 1)
 
     return (
         hidden_out,
@@ -609,9 +635,9 @@
         mine[1],
         mine[2],
         mine[3],
-        a_grad[:, :qcols],
+        qkv_grad,
         qb_grad,
-        a_grad[:, qcols : qcols + acols].T,
+        dense_grad,
         mine[4],
         b_grad[:, :fcols],
         ub_grad,

time: 194 us -> 207 us (1.067)
  waiting for transfers between devices: 71.6 us -> 88.8 us
  other arithmetic: 12.2 us -> 8.63 us
    ppermute x40, waiting for transfers between devices: 71.6 us -> 88.8 us  [swap(): return lax.ppermute(array, axis, [(i, i ^ bits) for i in range(size)])]
    unnamed x39 -> x38, local copies, waits for them, and re-layouts: 6.39 us -> 8.17 us
    pallas_call x11 -> x12, Pallas kernels: 51.5 us -> 51.6 us  [call(): pl.pallas_call(body, grid_spec=pltpu.PrefetchScalarGridSpec(num_scalar_pr...]
  transfers between devices with their start and end apart: 40 -> 40, of which waited for: 17 -> 18; matrix products, arithmetic and copies ran while one was open for 9% -> 6% of each run, Pallas kernels for 29% -> 20%
where the time goes in v1:
time: 207 us; the launch traced here: 204 us
  waiting for transfers between devices  88.8 us (43%)
  Pallas kernels  54.9 us (27%)
  starting transfers between devices  38.2 us (18%)
  local copies, waits for them, and re-layouts  12.4 us (6%)
  other arithmetic  8.63 us (4%)
    ppermute x40, waiting for transfers between devices, swap(): return lax.ppermute(array, axis, [(i, i ^ bits) for i in range(size)])  88.8 us
    pallas_call x12, Pallas kernels, call(): pl.pallas_call(body, grid_spec=pltpu.PrefetchScalarGridSpec(num_scalar_pr...  51.6 us
    ppermute x40, starting transfers between devices, swap(): return lax.ppermute(array, axis, [(i, i ^ bits) for i in range(size)])  38.2 us
    unnamed x38, local copies, waits for them, and re-layouts  8.17 us
  transfers between devices with their start and end apart: 40, of which 18 were waited for; matrix products, arithmetic and copies ran while one was open for 6% of the time, Pallas kernels for 20%

profile of v1, /device:TPU:0, one launch (start us, length us, event | category | flops | bytes accessed | tf_op | source)
XLA Modules:
  0.0 204.2 jit_solution(13316860172357095421)
XLA Ops:
  1.5 3.1 %collective-permute-start.3 = (f32[6,24]{1,0:T(8,128)S(1)}, f32[6,24]{1,0:T(8,128)S(1)}, u32[]{:S(2)}, u32[]{:S(2)}) collective-permute-start(f32[6,24]{1,0:T(8,128)S(1)} %stack.45), channel_id=1, source_target_pairs={{0,1},{1,0},{2,3},{3,2},{4,5},{5,4},{6,7},{7,6},{8,9},{9,8},{10,11... | collective-permute-start | bytes 1736 | tf_op jit(solution)/shard_map/ppermute | solution.py:49
  4.6 2.6 %collective-permute-start.2 = (f32[6,24]{1,0:T(8,128)S(1)}, f32[6,24]{1,0:T(8,128)S(1)}, u32[]{:S(2)}, u32[]{:S(2)}) collective-permute-start(f32[6,24]{1,0:T(8,128)S(1)} %stack.45), channel_id=1, source_target_pairs={{0,2},{1,3},{2,0},{3,1},{4,6},{5,7},{6,4},{7,5},{8,10},{9,11},{10,... | collective-permute-start | bytes 1736 | tf_op jit(solution)/shard_map/ppermute | solution.py:49
  10.8 1.8 collective-permute-done.1
  13.8 2.5 %collective-permute-start.6 = (bf16[112,768]{1,0:T(8,128)(2,1)S(1)}, bf16[112,768]{1,0:T(8,128)(2,1)S(1)}, u32[]{:S(2)}, u32[]{:S(2)}) collective-permute-start(bf16[112,768]{1,0:T(8,128)(2,1)S(1)} %pad_maximum_fusion.2.refs_0_), channel_id=1, source_target_pairs={{0,24},{4,28},{8,16},{12,20},{16,8},{20,12},{24,0},{28,4},{1,25},{... | collective-permute-start | bytes 516104 | tf_op jit(solution)/shard_map/ppermute | solution.py:49
  17.3 4.3 %collective-permute-done.6.refs_3_ = bf16[112,768]{1,0:T(8,128)(2,1)S(1)} collective-permute-done((bf16[112,768]{1,0:T(8,128)(2,1)S(1)}, bf16[112,768]{1,0:T(8,128)(2,1)S(1)}, u32[]{:S(2)}, u32[]{:S(2)}) %collective-permute-start.6) | collective-permute-done | bytes 172064 | tf_op jit(solution)/shard_map/ppermute | solution.py:49
  21.6 1.8 collective-permute-done.5.refs_2_
  24.8 3.5 %collective-permute-start.19 = (bf16[256,768]{1,0:T(8,128)(2,1)}, bf16[256,768]{1,0:T(8,128)(2,1)}, u32[]{:S(2)}, u32[]{:S(2)}) collective-permute-start(bf16[256,768]{1,0:T(8,128)(2,1)} %hid.1), channel_id=1, source_target_pairs={{0,2},{1,3},{2,0},{3,1},{4,6},{5,7},{6,4},{7,5},{8,10},{9,11},{10,... | collective-permute-start | bytes 1179656 | tf_op jit(solution)/shard_map/ppermute | solution.py:49
  29.4 1.8 collective-permute-start.13
  31.2 1.2 collective-permute-start.12
  32.9 1.0 fusion.10
  34.9 2.6 %shard_map.254 = (bf16[768,768]{1,0:T(8,128)(2,1)S(1)}, f32[6,768]{1,0:T(8,128)S(1)}, f32[1,576]{1,0:T(1,128)S(1)}, f32[1,768]{1,0:T(1,128)S(1)}) custom-call(s32[1]{0:T(128)} %bitcast.1.place, bf16[112,768]{1,0:T(8,128)(2,1)S(1)} %pad_maximum_fusion.2.refs_0_, bf16[112,768]{1,0:T(8,128)(2,1)S(1)} %collective-permute-done.4.refs_1_, ...), custom_call_target="tpu_custom_call" | custom-call | tf_op jit(solution)/shard_map/pallas_call | solution.py:124
  37.5 2.7 %collective-permute-done.13.refs_3_ = bf16[96,1536]{1,0:T(8,128)(2,1)S(1)} collective-permute-done((bf16[96,1536]{1,0:T(8,128)(2,1)S(1)}, bf16[96,1536]{1,0:T(8,128)(2,1)S(1)}, u32[]{:S(2)}, u32[]{:S(2)}) %collective-permute-start.13) | collective-permute-done | bytes 294944 | tf_op jit(solution)/shard_map/ppermute | solution.py:49
  40.3 4.8 %collective-permute-done.12.refs_2_ = bf16[96,1536]{1,0:T(8,128)(2,1)S(1)} collective-permute-done((bf16[96,1536]{1,0:T(8,128)(2,1)S(1)}, bf16[96,1536]{1,0:T(8,128)(2,1)S(1)}, u32[]{:S(2)}, u32[]{:S(2)}) %collective-permute-start.12) | collective-permute-done | bytes 294944 | tf_op jit(solution)/shard_map/ppermute | solution.py:49
  45.7 9.2 %collective-permute-done.19.hid_a = bf16[256,768]{1,0:T(8,128)(2,1)} collective-permute-done((bf16[256,768]{1,0:T(8,128)(2,1)}, bf16[256,768]{1,0:T(8,128)(2,1)}, u32[]{:S(2)}, u32[]{:S(2)}) %collective-permute-start.19) | collective-permute-done | bytes 393248 | tf_op jit(solution)/shard_map/ppermute | solution.py:49
  55.1 7.7 %shard_map.255 = (bf16[512,768]{1,0:T(8,128)(2,1)S(1)}, bf16[512,768]{1,0:T(8,128)(2,1)S(1)}, bf16[512,768]{1,0:T(8,128)(2,1)S(1)}, bf16[512,640]{1,0:T(8,128)(2...) custom-call(s32[2]{0:T(128)S(1)} %pad_add_fusion.meta.refs_0_, ...), custom_call_target="tpu_custom_call" | custom-call | flops 7000000000 | bytes 7168256 | tf_op jit(solution)/shard_map/pallas_call | solution.py:410
  63.1 1.7 collective-permute-start.23
  65.8 3.0 %shard_map.257 = (bf16[512,768]{1,0:T(8,128)(2,1)S(1)}, bf16[512,768]{1,0:T(8,128)(2,1)S(1)}, bf16[256,768]{1,0:T(8,128)(2,1)S(1)}, bf16[256,768]{1,0:T(8,128)(2,1)S(1)}) custom-call(s32[2]{0:T(128)S(1)} %pad_add_fusion.meta.refs_0_, bf16[512,768]{1,0:T(8,128)(2,1)S(1)} %get-tuple-element.72.second, bf16[512,192]{1,0:T(8,128)(2,1)S(1)} %get-tuple-element.73.att.refs_5_, ...), custom_call_target="tpu_custom_call" | custom-call | flops 3000000000 | bytes 6884352 | tf_op jit(solution)/shard_map/pallas_call | solution.py:410
  70.3 1.2 collective-permute-done.20.hid_b
  71.5 7.8 %shard_map.258 = (bf16[512,768]{1,0:T(8,128)(2,1)S(1)}, bf16[512,768]{1,0:T(8,128)(2,1)S(1)}, bf16[512,768]{1,0:T(8,128)(2,1)S(1)}, bf16[512,640]{1,0:T(8,128)(2...) custom-call(s32[2]{0:T(128)S(1)} %pad_add_fusion.meta.refs_0_, ...), custom_call_target="tpu_custom_call" | custom-call | flops 7000000000 | bytes 7168256 | tf_op jit(solution)/shard_map/pallas_call | solution.py:410
  79.3 3.9 %shard_map.259 = (bf16[512,768]{1,0:T(8,128)(2,1)S(1)}, bf16[512,768]{1,0:T(8,128)(2,1)S(1)}, bf16[256,768]{1,0:T(8,128)(2,1)S(1)}, bf16[256,768]{1,0:T(8,128)(2,1)}) custom-call(s32[2]{0:T(128)S(1)} %pad_add_fusion.meta.refs_0_, bf16[512,768]{1,0:T(8,128)(2,1)S(1)} %get-tuple-element.77.second, bf16[512,192]{1,0:T(8,128)(2,1)S(1)} %get-tuple-element.78.att.refs_5_, ...), custom_call_target="tpu_custom_call" | custom-call | flops 3000000000 | bytes 6884352 | tf_op jit(solution)/shard_map/pallas_call | solution.py:410
  83.9 4.3 %collective-permute-done.25.cot_b.refs_2_ = bf16[256,768]{1,0:T(8,128)(2,1)S(1)} collective-permute-done((bf16[256,768]{1,0:T(8,128)(2,1)S(1)}, bf16[256,768]{1,0:T(8,128)(2,1)S(1)}, u32[]{:S(2)}, u32[]{:S(2)}) %collective-permute-start.25) | collective-permute-done | bytes 393248 | tf_op jit(solution)/shard_map/ppermute | solution.py:49
  88.3 3.3 %shard_map.261 = (bf16[512,768]{1,0:T(8,128)(2,1)S(1)}, f32[768,768]{1,0:T(8,128)S(1)}, f32[768,768]{1,0:T(8,128)S(1)}, f32[8,768]{1,0:T(8,128)S(1)}, f32[8,768]{1,0:T(8,128)S(1)}) custom-call(s32[2]{0:T(128)S(1)} %pad_add_fusion.meta.refs_0_, bf16[256,768]{1,0:T(8,128)(2,1)S(1)} %collective-permute-done.24.cot_a.refs_1_, ...), custom_call_target="tpu_custom_call" | custom-call | flops 5000000000 | bytes 11864064 | tf_op jit(solution)/shard_map/pallas_call | solution.py:410
  91.6 8.0 %shard_map.263 = (bf16[256,768]{1,0:T(8,128)(2,1)S(1)}, bf16[256,768]{1,0:T(8,128)(2,1)S(1)}, f32[8,768]{1,0:T(8,128)S(1)}, f32[8,640]{1,0:T(8,128)S(1)}, f32[76...) custom-call(s32[2]{0:T(128)S(1)} %pad_add_fusion.meta.refs_0_, bf16[256,768]{1,0:T(8,128)(2,1)S(1)} %collective-permute-done.24.cot_a.refs_1_, ...), custom_call_target="tpu_custom_call" | custom-call | flops 8999999488 | bytes 10352640 | tf_op jit(solution)/shard_map/pallas_call | solution.py:410
  101.1 3.6 %shard_map.262 = (bf16[512,768]{1,0:T(8,128)(2,1)S(1)}, f32[4,96,1536]{2,1,0:T(8,128)S(1)}, bf16[4,96,1536]{2,1,0:T(8,128)(2,1)S(1)}, f32[8,768]{1,0:T(8,128)S(1)}, f32[8,768]{1,0:T(8,128)S(1)}) custom-call(s32[2]{0:T(128)S(1)} %pad_add_fusion.meta.refs_0_, bf16[256,768]{1,0:T(8,128)(2,1)S(1)} %get-tuple-element.81.cot_a.refs_1_, ...), custom_call_target="tpu_custom_call" | custom-call | flops 5000000000 | bytes 15452160 | tf_op jit(solution)/shard_map/pallas_call | solution.py:410
  105.8 8.3 %shard_map.264 = (bf16[256,768]{1,0:T(8,128)(2,1)S(1)}, bf16[256,768]{1,0:T(8,128)(2,1)S(1)}, f32[8,768]{1,0:T(8,128)S(1)}, f32[8,640]{1,0:T(8,128)S(1)}, f32[76...) custom-call(s32[2]{0:T(128)S(1)} %pad_add_fusion.meta.refs_0_, bf16[256,768]{1,0:T(8,128)(2,1)S(1)} %get-tuple-element.81.cot_a.refs_1_, ...), custom_call_target="tpu_custom_call" | custom-call | flops 8999999488 | bytes 12756992 | tf_op jit(solution)/shard_map/pallas_call | solution.py:410
  114.1 1.9 shard_map.266
  116.0 1.1 copy-done
  117.1 2.0 collective-permute-start.18
  119.2 2.0 collective-permute-start.27
  121.2 8.2 %collective-permute-done.21 = bf16[256,768]{1,0:T(8,128)(2,1)} collective-permute-done((bf16[256,768]{1,0:T(8,128)(2,1)}, bf16[256,768]{1,0:T(8,128)(2,1)}, u32[]{:S(2)}, u32[]{:S(2)}) %collective-permute-start.21) | collective-permute-done | bytes 393248 | tf_op jit(solution)/shard_map/ppermute | solution.py:49
  129.4 1.2 add_convert_fusion.1
  130.7 1.0 collective-permute-start.22
  131.7 1.7 fusion.13
  133.4 29.2 %collective-permute-done.27 = bf16[256,768]{1,0:T(8,128)(2,1)S(1)} collective-permute-done((bf16[256,768]{1,0:T(8,128)(2,1)}, bf16[256,768]{1,0:T(8,128)(2,1)S(1)}, u32[]{:S(2)}, u32[]{:S(2)}) %collective-permute-start.27) | collective-permute-done | bytes 393248 | tf_op jit(solution)/shard_map/ppermute | solution.py:49
  162.6 1.5 collective-permute-start.32
  166.5 2.0 collective-permute-done.32.got_c
  168.5 1.7 collective-permute-start.30
  170.1 1.1 add_add_fusion
  171.6 3.3 %collective-permute-done.30.got_a = bf16[96,896]{1,0:T(8,128)(2,1)S(1)} collective-permute-done((bf16[96,896]{1,0:T(8,128)(2,1)S(1)}, bf16[96,896]{1,0:T(8,128)(2,1)S(1)}, u32[]{:S(2)}, u32[]{:S(2)}) %collective-permute-start.30) | collective-permute-done | bytes 172064 | tf_op jit(solution)/shard_map/ppermute | solution.py:49
  174.8 1.5 shard_map.267
  176.3 2.4 %collective-permute-start.35 = (f32[8,128]{1,0:T(8,128)S(1)}, f32[8,128]{1,0:T(8,128)S(1)}, u32[]{:S(2)}, u32[]{:S(2)}) collective-permute-start(f32[8,128]{1,0:T(8,128)S(1)} %get-tuple-element.117), channel_id=1, source_target_pairs={{0,3},{1,2},{2,1},{3,0},{4,7},{5,6},{6,5},{7,4},{8,11},{9,10},{10,... | collective-permute-start | bytes 12296 | tf_op jit(solution)/shard_map/ppermute | solution.py:49
  178.7 1.4 collective-permute-start.34
  180.7 3.3 %collective-permute-done.28.two = bf16[256,768]{1,0:T(8,128)(2,1)S(1)} collective-permute-done((bf16[256,768]{1,0:T(8,128)(2,1)S(1)}, bf16[256,768]{1,0:T(8,128)(2,1)S(1)}, u32[]{:S(2)}, u32[]{:S(2)}) %collective-permute-start.28) | collective-permute-done | bytes 393248 | tf_op jit(solution)/shard_map/ppermute | solution.py:49
  184.0 2.0 shard_map.265
  186.3 1.6 collective-permute-start.37
  188.6 1.3 collective-permute-start.38
  190.5 6.7 %collective-permute-done.37 = bf16[96,1536]{1,0:T(8,128)(2,1)S(1)} collective-permute-done((bf16[96,1536]{1,0:T(8,128)(2,1)S(1)}, bf16[96,1536]{1,0:T(8,128)(2,1)S(1)}, u32[]{:S(2)}, u32[]{:S(2)}) %collective-permute-start.37) | collective-permute-done | bytes 294944 | tf_op jit(solution)/shard_map/ppermute | solution.py:49
  197.2 5.2 %collective-permute-done.39 = bf16[96,1536]{1,0:T(8,128)(2,1)S(1)} collective-permute-done((bf16[96,1536]{1,0:T(8,128)(2,1)S(1)}, bf16[96,1536]{1,0:T(8,128)(2,1)S(1)}, u32[]{:S(2)}, u32[]{:S(2)}) %collective-permute-start.39) | collective-permute-done | bytes 294944 | tf_op jit(solution)/shard_map/ppermute | solution.py:49
  (114 shorter events, 23.9 us)
Async XLA Ops:
  0.6 28.1 %copy-start.1 = (f32[256,768]{1,0:T(8,128)S(1)}, f32[256,768]{1,0:T(8,128)}, u32[]{:S(2)}) copy-start(f32[256,768]{1,0:T(8,128)} %cot.3) | copy-start | bytes 2359300
  1.5 9.3 %collective-permute-start.3 = (f32[6,24]{1,0:T(8,128)S(1)}, f32[6,24]{1,0:T(8,128)S(1)}, u32[]{:S(2)}, u32[]{:S(2)}) collective-permute-start(f32[6,24]{1,0:T(8,128)S(1)} %stack.45), channel_id=1, source_target_pairs={{0,1},{1,0},{2,3},{3,2},{4,5},{5,4},{6,7},{7,6},{8,9},{9,8},{10,11... | collective-permute-start | bytes 1736 | tf_op jit(solution)/shard_map/ppermute | solution.py:49
  4.6 6.2 %collective-permute-start.2 = (f32[6,24]{1,0:T(8,128)S(1)}, f32[6,24]{1,0:T(8,128)S(1)}, u32[]{:S(2)}, u32[]{:S(2)}) collective-permute-start(f32[6,24]{1,0:T(8,128)S(1)} %stack.45), channel_id=1, source_target_pairs={{0,2},{1,3},{2,0},{3,1},{4,6},{5,7},{6,4},{7,5},{8,10},{9,11},{10,... | collective-permute-start | bytes 1736 | tf_op jit(solution)/shard_map/ppermute | solution.py:49
  7.2 5.4 %collective-permute-start.1 = (f32[6,24]{1,0:T(8,128)S(1)}, f32[6,24]{1,0:T(8,128)S(1)}, u32[]{:S(2)}, u32[]{:S(2)}) collective-permute-start(f32[6,24]{1,0:T(8,128)S(1)} %stack.45), channel_id=1, source_target_pairs={{0,3},{1,2},{2,1},{3,0},{4,7},{5,6},{6,5},{7,4},{8,11},{9,10},{10,... | collective-permute-start | bytes 1736 | tf_op jit(solution)/shard_map/ppermute | solution.py:49
  8.2 16.6 %collective-permute-start.14 = (bf16[96,1536]{1,0:T(8,128)(2,1)S(1)}, bf16[96,1536]{1,0:T(8,128)(2,1)S(1)}, u32[]{:S(2)}, u32[]{:S(2)}) collective-permute-start(bf16[96,1536]{1,0:T(8,128)(2,1)S(1)} %pad_maximum_fusion.1.refs_0_), channel_id=1, source_target_pairs={{0,4},{4,0},{8,12},{12,8},{16,20},{20,16},{24,28},{28,24},{1,5},{5... | collective-permute-start | bytes 884744 | tf_op jit(solution)/shard_map/ppermute | solution.py:49
  13.8 7.9 %collective-permute-start.6 = (bf16[112,768]{1,0:T(8,128)(2,1)S(1)}, bf16[112,768]{1,0:T(8,128)(2,1)S(1)}, u32[]{:S(2)}, u32[]{:S(2)}) collective-permute-start(bf16[112,768]{1,0:T(8,128)(2,1)S(1)} %pad_maximum_fusion.2.refs_0_), channel_id=1, source_target_pairs={{0,24},{4,28},{8,16},{12,20},{16,8},{20,12},{24,0},{28,4},{1,25},{... | collective-permute-start | bytes 516104 | tf_op jit(solution)/shard_map/ppermute | solution.py:49
  16.3 7.1 %collective-permute-start.5 = (bf16[112,768]{1,0:T(8,128)(2,1)S(1)}, bf16[112,768]{1,0:T(8,128)(2,1)S(1)}, u32[]{:S(2)}, u32[]{:S(2)}) collective-permute-start(bf16[112,768]{1,0:T(8,128)(2,1)S(1)} %pad_maximum_fusion.2.refs_0_), channel_id=1, source_target_pairs={{0,16},{4,20},{8,24},{12,28},{16,0},{20,4},{24,8},{28,12},{1,17},{... | collective-permute-start | bytes 516104 | tf_op jit(solution)/shard_map/ppermute | solution.py:49
  16.8 6.9 %collective-permute-start.4 = (bf16[112,768]{1,0:T(8,128)(2,1)S(1)}, bf16[112,768]{1,0:T(8,128)(2,1)S(1)}, u32[]{:S(2)}, u32[]{:S(2)}) collective-permute-start(bf16[112,768]{1,0:T(8,128)(2,1)S(1)} %pad_maximum_fusion.2.refs_0_), channel_id=1, source_target_pairs={{0,8},{4,12},{8,0},{12,4},{16,24},{20,28},{24,16},{28,20},{1,9},{5... | collective-permute-start | bytes 516104 | tf_op jit(solution)/shard_map/ppermute | solution.py:49
  17.3 6.6 %collective-permute-start.7 = (bf16[112,768]{1,0:T(8,128)(2,1)S(1)}, bf16[112,768]{1,0:T(8,128)(2,1)S(1)}, u32[]{:S(2)}, u32[]{:S(2)}) collective-permute-start(bf16[112,768]{1,0:T(8,128)(2,1)S(1)} %pad_maximum_fusion.2.refs_0_), channel_id=1, source_target_pairs={{0,4},{4,0},{8,12},{12,8},{16,20},{20,16},{24,28},{28,24},{1,5},{5... | collective-permute-start | bytes 516104 | tf_op jit(solution)/shard_map/ppermute | solution.py:49
  21.6 7.7 %collective-permute-start.10 = (bf16[112,768]{1,0:T(8,128)(2,1)S(1)}, bf16[112,768]{1,0:T(8,128)(2,1)S(1)}, u32[]{:S(2)}, u32[]{:S(2)}) collective-permute-start(bf16[112,768]{1,0:T(8,128)(2,1)S(1)} %collective-permute-done.6.refs_3_), channel_id=1, source_target_pairs={{0,4},{4,0},{8,12},{12,8},{16,20},{20,16},{24,28},{28,24},{1,5},{5... | collective-permute-start | bytes 516104 | tf_op jit(solution)/shard_map/ppermute | solution.py:49
  23.4 7.8 %collective-permute-start.9 = (bf16[112,768]{1,0:T(8,128)(2,1)S(1)}, bf16[112,768]{1,0:T(8,128)(2,1)S(1)}, u32[]{:S(2)}, u32[]{:S(2)}) collective-permute-start(bf16[112,768]{1,0:T(8,128)(2,1)S(1)} %collective-permute-done.5.refs_2_), channel_id=1, source_target_pairs={{0,4},{4,0},{8,12},{12,8},{16,20},{20,16},{24,28},{28,24},{1,5},{5... | collective-permute-start | bytes 516104 | tf_op jit(solution)/shard_map/ppermute | solution.py:49
  23.6 8.8 %collective-permute-start.8 = (bf16[112,768]{1,0:T(8,128)(2,1)S(1)}, bf16[112,768]{1,0:T(8,128)(2,1)S(1)}, u32[]{:S(2)}, u32[]{:S(2)}) collective-permute-start(bf16[112,768]{1,0:T(8,128)(2,1)S(1)} %collective-permute-done.4.refs_1_), channel_id=1, source_target_pairs={{0,4},{4,0},{8,12},{12,8},{16,20},{20,16},{24,28},{28,24},{1,5},{5... | collective-permute-start | bytes 516104 | tf_op jit(solution)/shard_map/ppermute | solution.py:49
  23.9 21.7 %collective-permute-start = (bf16[256,768]{1,0:T(8,128)(2,1)}, bf16[256,768]{1,0:T(8,128)(2,1)}, u32[]{:S(2)}, u32[]{:S(2)}) collective-permute-start(bf16[256,768]{1,0:T(8,128)(2,1)} %hid.1), channel_id=1, source_target_pairs={{0,1},{1,0},{2,3},{3,2},{4,5},{5,4},{6,7},{7,6},{8,9},{9,8},{10,11... | collective-permute-start | bytes 1179656 | tf_op jit(solution)/shard_map/ppermute | solution.py:49
  24.8 30.1 %collective-permute-start.19 = (bf16[256,768]{1,0:T(8,128)(2,1)}, bf16[256,768]{1,0:T(8,128)(2,1)}, u32[]{:S(2)}, u32[]{:S(2)}) collective-permute-start(bf16[256,768]{1,0:T(8,128)(2,1)} %hid.1), channel_id=1, source_target_pairs={{0,2},{1,3},{2,0},{3,1},{4,6},{5,7},{6,4},{7,5},{8,10},{9,11},{10,... | collective-permute-start | bytes 1179656 | tf_op jit(solution)/shard_map/ppermute | solution.py:49
  29.4 10.9 %collective-permute-start.13 = (bf16[96,1536]{1,0:T(8,128)(2,1)S(1)}, bf16[96,1536]{1,0:T(8,128)(2,1)S(1)}, u32[]{:S(2)}, u32[]{:S(2)}) collective-permute-start(bf16[96,1536]{1,0:T(8,128)(2,1)S(1)} %pad_maximum_fusion.1.refs_0_), channel_id=1, source_target_pairs={{0,24},{4,28},{8,16},{12,20},{16,8},{20,12},{24,0},{28,4},{1,25},{... | collective-permute-start | bytes 884744 | tf_op jit(solution)/shard_map/ppermute | solution.py:49
  31.2 13.9 %collective-permute-start.12 = (bf16[96,1536]{1,0:T(8,128)(2,1)S(1)}, bf16[96,1536]{1,0:T(8,128)(2,1)S(1)}, u32[]{:S(2)}, u32[]{:S(2)}) collective-permute-start(bf16[96,1536]{1,0:T(8,128)(2,1)S(1)} %pad_maximum_fusion.1.refs_0_), channel_id=1, source_target_pairs={{0,16},{4,20},{8,24},{12,28},{16,0},{20,4},{24,8},{28,12},{1,17},{... | collective-permute-start | bytes 884744 | tf_op jit(solution)/shard_map/ppermute | solution.py:49
  32.4 12.8 %collective-permute-start.11 = (bf16[96,1536]{1,0:T(8,128)(2,1)S(1)}, bf16[96,1536]{1,0:T(8,128)(2,1)S(1)}, u32[]{:S(2)}, u32[]{:S(2)}) collective-permute-start(bf16[96,1536]{1,0:T(8,128)(2,1)S(1)} %pad_maximum_fusion.1.refs_0_), channel_id=1, source_target_pairs={{0,8},{4,12},{8,0},{12,4},{16,24},{20,28},{24,16},{28,20},{1,9},{5... | collective-permute-start | bytes 884744 | tf_op jit(solution)/shard_map/ppermute | solution.py:49
  34.0 21.1 %copy-start.2 = (bf16[256,768]{1,0:T(8,128)(2,1)S(1)}, bf16[256,768]{1,0:T(8,128)(2,1)}, u32[]{:S(2)}) copy-start(bf16[256,768]{1,0:T(8,128)(2,1)} %hid.1) | copy-start | bytes 1179652
  37.5 68.2 %copy-start.10 = (f32[6,768]{1,0:T(8,128)}, f32[6,768]{1,0:T(8,128)S(1)}, u32[]{:S(2)}) copy-start(f32[6,768]{1,0:T(8,128)S(1)} %get-tuple-element.69.gains.refs_9_) | copy-start | bytes 55300
  40.3 22.8 %collective-permute-start.24 = (bf16[256,768]{1,0:T(8,128)(2,1)S(1)}, bf16[256,768]{1,0:T(8,128)(2,1)S(1)}, u32[]{:S(2)}, u32[]{:S(2)}) collective-permute-start(bf16[256,768]{1,0:T(8,128)(2,1)S(1)} %get-tuple-element.81.cot_a.refs_1_), channel_id=1, source_target_pairs={{0,2},{1,3},{2,0},{3,1},{4,6},{5,7},{6,4},{7,5},{8,10},{9,11},{10,... | collective-permute-start | bytes 1179656 | tf_op jit(solution)/shard_map/ppermute | solution.py:49
  45.1 19.7 %collective-permute-start.17 = (bf16[96,1536]{1,0:T(8,128)(2,1)S(1)}, bf16[96,1536]{1,0:T(8,128)(2,1)S(1)}, u32[]{:S(2)}, u32[]{:S(2)}) collective-permute-start(bf16[96,1536]{1,0:T(8,128)(2,1)S(1)} %collective-permute-done.13.refs_3_), channel_id=1, source_target_pairs={{0,4},{4,0},{8,12},{12,8},{16,20},{20,16},{24,28},{28,24},{1,5},{5... | collective-permute-start | bytes 884744 | tf_op jit(solution)/shard_map/ppermute | solution.py:49
  45.2 19.9 %collective-permute-start.16 = (bf16[96,1536]{1,0:T(8,128)(2,1)S(1)}, bf16[96,1536]{1,0:T(8,128)(2,1)S(1)}, u32[]{:S(2)}, u32[]{:S(2)}) collective-permute-start(bf16[96,1536]{1,0:T(8,128)(2,1)S(1)} %collective-permute-done.12.refs_2_), channel_id=1, source_target_pairs={{0,4},{4,0},{8,12},{12,8},{16,20},{20,16},{24,28},{28,24},{1,5},{5... | collective-permute-start | bytes 884744 | tf_op jit(solution)/shard_map/ppermute | solution.py:49
  45.6 19.5 %collective-permute-start.15 = (bf16[96,1536]{1,0:T(8,128)(2,1)S(1)}, bf16[96,1536]{1,0:T(8,128)(2,1)S(1)}, u32[]{:S(2)}, u32[]{:S(2)}) collective-permute-start(bf16[96,1536]{1,0:T(8,128)(2,1)S(1)} %collective-permute-done.11.refs_1_), channel_id=1, source_target_pairs={{0,4},{4,0},{8,12},{12,8},{16,20},{20,16},{24,28},{28,24},{1,5},{5... | collective-permute-start | bytes 884744 | tf_op jit(solution)/shard_map/ppermute | solution.py:49
  54.9 16.6 %collective-permute-start.20 = (bf16[256,768]{1,0:T(8,128)(2,1)}, bf16[256,768]{1,0:T(8,128)(2,1)S(1)}, u32[]{:S(2)}, u32[]{:S(2)}) collective-permute-start(bf16[256,768]{1,0:T(8,128)(2,1)} %collective-permute-done.19.hid_a), channel_id=1, source_target_pairs={{0,1},{1,0},{2,3},{3,2},{4,5},{5,4},{6,7},{7,6},{8,9},{9,8},{10,11... | collective-permute-start | bytes 1179656 | tf_op jit(solution)/shard_map/ppermute | solution.py:49
  63.1 38.0 %collective-permute-start.23 = (bf16[256,768]{1,0:T(8,128)(2,1)S(1)}, bf16[256,768]{1,0:T(8,128)(2,1)S(1)}, u32[]{:S(2)}, u32[]{:S(2)}) collective-permute-start(bf16[256,768]{1,0:T(8,128)(2,1)S(1)} %get-tuple-element.81.cot_a.refs_1_), channel_id=1, source_target_pairs={{0,1},{1,0},{2,3},{3,2},{4,5},{5,4},{6,7},{7,6},{8,9},{9,8},{10,11... | collective-permute-start | bytes 1179656 | tf_op jit(solution)/shard_map/ppermute | solution.py:49
  64.8 23.5 %collective-permute-start.25 = (bf16[256,768]{1,0:T(8,128)(2,1)S(1)}, bf16[256,768]{1,0:T(8,128)(2,1)S(1)}, u32[]{:S(2)}, u32[]{:S(2)}) collective-permute-start(bf16[256,768]{1,0:T(8,128)(2,1)S(1)} %collective-permute-done.24.cot_a.refs_1_), channel_id=1, source_target_pairs={{0,1},{1,0},{2,3},{3,2},{4,5},{5,4},{6,7},{7,6},{8,9},{9,8},{10,11... | collective-permute-start | bytes 1179656 | tf_op jit(solution)/shard_map/ppermute | solution.py:49
  114.0 2.0 copy-start.13
  117.1 13.5 %collective-permute-start.29 = (bf16[4,96,896]{2,1,0:T(8,128)(2,1)}, bf16[4,96,896]{2,1,0:T(8,128)(2,1)}, u32[]{:S(2)}, u32[]{:S(2)}) collective-permute-start(bf16[4,96,896]{2,1,0:T(8,128)(2,1)} %get-tuple-element.116), channel_id=1, source_target_pairs={{0,4},{4,0},{8,12},{12,8},{16,20},{20,16},{24,28},{28,24},{1,5},{5... | collective-permute-start | bytes 2064392 | tf_op jit(solution)/shard_map/ppermute | solution.py:49
  117.1 12.3 %collective-permute-start.21 = (bf16[256,768]{1,0:T(8,128)(2,1)}, bf16[256,768]{1,0:T(8,128)(2,1)}, u32[]{:S(2)}, u32[]{:S(2)}) collective-permute-start(bf16[256,768]{1,0:T(8,128)(2,1)} %get-tuple-element.80), channel_id=1, source_target_pairs={{0,1},{1,0},{2,3},{3,2},{4,5},{5,4},{6,7},{7,6},{8,9},{9,8},{10,11... | collective-permute-start | bytes 1179656 | tf_op jit(solution)/shard_map/ppermute | solution.py:49
  117.1 47.0 %collective-permute-start.18 = (bf16[256,768]{1,0:T(8,128)(2,1)}, bf16[256,768]{1,0:T(8,128)(2,1)S(1)}, u32[]{:S(2)}, u32[]{:S(2)}) collective-permute-start(bf16[256,768]{1,0:T(8,128)(2,1)} %copy-done.12), channel_id=1, source_target_pairs={{0,1},{1,0},{2,3},{3,2},{4,5},{5,4},{6,7},{7,6},{8,9},{9,8},{10,11... | collective-permute-start | bytes 1179656 | tf_op jit(solution)/shard_map/ppermute | solution.py:49
  119.2 61.0 %collective-permute-start.26 = (bf16[256,768]{1,0:T(8,128)(2,1)}, bf16[256,768]{1,0:T(8,128)(2,1)S(1)}, u32[]{:S(2)}, u32[]{:S(2)}) collective-permute-start(bf16[256,768]{1,0:T(8,128)(2,1)} %copy-done.13), channel_id=1, source_target_pairs={{0,1},{1,0},{2,3},{3,2},{4,5},{5,4},{6,7},{7,6},{8,9},{9,8},{10,11... | collective-permute-start | bytes 1179656 | tf_op jit(solution)/shard_map/ppermute | solution.py:49
  119.2 43.4 %collective-permute-start.27 = (bf16[256,768]{1,0:T(8,128)(2,1)}, bf16[256,768]{1,0:T(8,128)(2,1)S(1)}, u32[]{:S(2)}, u32[]{:S(2)}) collective-permute-start(bf16[256,768]{1,0:T(8,128)(2,1)} %copy-done.14), channel_id=1, source_target_pairs={{0,1},{1,0},{2,3},{3,2},{4,5},{5,4},{6,7},{7,6},{8,9},{9,8},{10,11... | collective-permute-start | bytes 1179656 | tf_op jit(solution)/shard_map/ppermute | solution.py:49
  129.4 56.6 %collective-permute-start.36 = (bf16[4,96,1536]{2,1,0:T(8,128)(2,1)}, bf16[4,96,1536]{2,1,0:T(8,128)(2,1)S(1)}, u32[]{:S(2)}, u32[]{:S(2)}) collective-permute-start(bf16[4,96,1536]{2,1,0:T(8,128)(2,1)} %copy-done.11), channel_id=1, source_target_pairs={{0,4},{4,0},{8,12},{12,8},{16,20},{20,16},{24,28},{28,24},{1,5},{5... | collective-permute-start | bytes 3538952 | tf_op jit(solution)/shard_map/ppermute | solution.py:49
  130.7 35.0 %collective-permute-start.22 = (bf16[256,768]{1,0:T(8,128)(2,1)S(1)}, bf16[256,768]{1,0:T(8,128)(2,1)S(1)}, u32[]{:S(2)}, u32[]{:S(2)}) collective-permute-start(bf16[256,768]{1,0:T(8,128)(2,1)S(1)} %add_convert_fusion.1), channel_id=1, source_target_pairs={{0,2},{1,3},{2,0},{3,1},{4,6},{5,7},{6,4},{7,5},{8,10},{9,11},{10,... | collective-permute-start | bytes 1179656 | tf_op jit(solution)/shard_map/ppermute | solution.py:49
  131.7 32.3 %copy-start.6 = (bf16[256,768]{1,0:T(8,128)(2,1)S(1)}, bf16[256,768]{1,0:T(8,128)(2,1)}, u32[]{:S(2)}) copy-start(bf16[256,768]{1,0:T(8,128)(2,1)} %copy-done.5) | copy-start | bytes 1179652
  131.7 38.4 %copy-start.4 = (bf16[256,768]{1,0:T(8,128)(2,1)S(1)}, bf16[256,768]{1,0:T(8,128)(2,1)}, u32[]{:S(2)}) copy-start(bf16[256,768]{1,0:T(8,128)(2,1)} %copy-done.3) | copy-start | bytes 1179652
  162.6 5.9 %collective-permute-start.32 = (bf16[96,896]{1,0:T(8,128)(2,1)S(1)}, bf16[96,896]{1,0:T(8,128)(2,1)S(1)}, u32[]{:S(2)}, u32[]{:S(2)}) collective-permute-start(bf16[96,896]{1,0:T(8,128)(2,1)S(1)} %get-tuple-element.129), channel_id=1, source_target_pairs={{0,16},{4,20},{8,24},{12,28},{16,0},{20,4},{24,8},{28,12},{1,17},{... | collective-permute-start | bytes 516104 | tf_op jit(solution)/shard_map/ppermute | solution.py:49
  164.1 19.8 %collective-permute-start.28 = (bf16[256,768]{1,0:T(8,128)(2,1)S(1)}, bf16[256,768]{1,0:T(8,128)(2,1)S(1)}, u32[]{:S(2)}, u32[]{:S(2)}) collective-permute-start(bf16[256,768]{1,0:T(8,128)(2,1)S(1)} %add_convert_fusion), channel_id=1, source_target_pairs={{0,2},{1,3},{2,0},{3,1},{4,6},{5,7},{6,4},{7,5},{8,10},{9,11},{10,... | collective-permute-start | bytes 1179656 | tf_op jit(solution)/shard_map/ppermute | solution.py:49
  165.7 5.9 %collective-permute-start.31 = (bf16[96,896]{1,0:T(8,128)(2,1)S(1)}, bf16[96,896]{1,0:T(8,128)(2,1)S(1)}, u32[]{:S(2)}, u32[]{:S(2)}) collective-permute-start(bf16[96,896]{1,0:T(8,128)(2,1)S(1)} %get-tuple-element.130), channel_id=1, source_target_pairs={{0,8},{4,12},{8,0},{12,4},{16,24},{20,28},{24,16},{28,20},{1,9},{5... | collective-permute-start | bytes 516104 | tf_op jit(solution)/shard_map/ppermute | solution.py:49
  168.5 6.4 %collective-permute-start.30 = (bf16[96,896]{1,0:T(8,128)(2,1)S(1)}, bf16[96,896]{1,0:T(8,128)(2,1)S(1)}, u32[]{:S(2)}, u32[]{:S(2)}) collective-permute-start(bf16[96,896]{1,0:T(8,128)(2,1)S(1)} %get-tuple-element.131), channel_id=1, source_target_pairs={{0,24},{4,28},{8,16},{12,20},{16,8},{20,12},{24,0},{28,4},{1,25},{... | collective-permute-start | bytes 516104 | tf_op jit(solution)/shard_map/ppermute | solution.py:49
  174.8 9.1 %copy-start.16 = (bf16[256,768]{1,0:T(8,128)(2,1)S(1)}, bf16[256,768]{1,0:T(8,128)(2,1)}, u32[]{:S(2)}) copy-start(bf16[256,768]{1,0:T(8,128)(2,1)} %copy-done.15) | copy-start | bytes 1179652
  176.3 9.7 %collective-permute-start.35 = (f32[8,128]{1,0:T(8,128)S(1)}, f32[8,128]{1,0:T(8,128)S(1)}, u32[]{:S(2)}, u32[]{:S(2)}) collective-permute-start(f32[8,128]{1,0:T(8,128)S(1)} %get-tuple-element.117), channel_id=1, source_target_pairs={{0,3},{1,2},{2,1},{3,0},{4,7},{5,6},{6,5},{7,4},{8,11},{9,10},{10,... | collective-permute-start | bytes 12296 | tf_op jit(solution)/shard_map/ppermute | solution.py:49
  178.7 7.3 %collective-permute-start.34 = (f32[8,128]{1,0:T(8,128)S(1)}, f32[8,128]{1,0:T(8,128)S(1)}, u32[]{:S(2)}, u32[]{:S(2)}) collective-permute-start(f32[8,128]{1,0:T(8,128)S(1)} %get-tuple-element.117), channel_id=1, source_target_pairs={{0,2},{1,3},{2,0},{3,1},{4,6},{5,7},{6,4},{7,5},{8,10},{9,11},{10,... | collective-permute-start | bytes 12296 | tf_op jit(solution)/shard_map/ppermute | solution.py:49
  180.1 5.9 %collective-permute-start.33 = (f32[8,128]{1,0:T(8,128)S(1)}, f32[8,128]{1,0:T(8,128)S(1)}, u32[]{:S(2)}, u32[]{:S(2)}) collective-permute-start(f32[8,128]{1,0:T(8,128)S(1)} %get-tuple-element.117), channel_id=1, source_target_pairs={{0,1},{1,0},{2,3},{3,2},{4,5},{5,4},{6,7},{7,6},{8,9},{9,8},{10,11... | collective-permute-start | bytes 12296 | tf_op jit(solution)/shard_map/ppermute | solution.py:49
  186.3 10.9 %collective-permute-start.37 = (bf16[96,1536]{1,0:T(8,128)(2,1)S(1)}, bf16[96,1536]{1,0:T(8,128)(2,1)S(1)}, u32[]{:S(2)}, u32[]{:S(2)}) collective-permute-start(bf16[96,1536]{1,0:T(8,128)(2,1)S(1)} %get-tuple-element.126), channel_id=1, source_target_pairs={{0,24},{4,28},{8,16},{12,20},{16,8},{20,12},{24,0},{28,4},{1,25},{... | collective-permute-start | bytes 884744 | tf_op jit(solution)/shard_map/ppermute | solution.py:49
  187.9 14.6 %collective-permute-start.39 = (bf16[96,1536]{1,0:T(8,128)(2,1)S(1)}, bf16[96,1536]{1,0:T(8,128)(2,1)S(1)}, u32[]{:S(2)}, u32[]{:S(2)}) collective-permute-start(bf16[96,1536]{1,0:T(8,128)(2,1)S(1)} %get-tuple-element.127), channel_id=1, source_target_pairs={{0,16},{4,20},{8,24},{12,28},{16,0},{20,4},{24,8},{28,12},{1,17},{... | collective-permute-start | bytes 884744 | tf_op jit(solution)/shard_map/ppermute | solution.py:49
  188.6 13.8 %collective-permute-start.38 = (bf16[96,1536]{1,0:T(8,128)(2,1)S(1)}, bf16[96,1536]{1,0:T(8,128)(2,1)S(1)}, u32[]{:S(2)}, u32[]{:S(2)}) collective-permute-start(bf16[96,1536]{1,0:T(8,128)(2,1)S(1)} %get-tuple-element.128), channel_id=1, source_target_pairs={{0,8},{4,12},{8,0},{12,4},{16,24},{20,28},{24,16},{28,20},{1,9},{5... | collective-permute-start | bytes 884744 | tf_op jit(solution)/shard_map/ppermute | solution.py:49
  190.4 13.0 %copy-start.17 = (f32[24]{0:T(128)}, f32[24]{0:T(128)S(1)}, u32[]{:S(2)}) copy-start(f32[24]{0:T(128)S(1)} %get-tuple-element.185) | copy-start | bytes 292
  (10 other events, 10.4 us)
